TPU v7x, 128 devices: a whole 4x4x4 slice. The times are simulated.
128 devices in a mesh: dp: 32 (over z_lo, x, y), tensor: 4 (over z_hi, core).
Axes of the slice: x: 4, y: 4, z: 4 (z_hi: 2, z_lo: 2; z = z_hi * 2 + z_lo), core: 2. Of those that a mesh axis runs over, the one named last changes fastest.
Arguments:
- hidden: bfloat16 [64, 512, 5120], P('dp'), may hold values from -5 to 5
- query_projection_matrix: bfloat16 [5120, 2560], P('dp', 'tensor'), may hold values from -0.5 to 0.5
- key_projection_matrix: bfloat16 [5120, 2560], P('dp', 'tensor'), may hold values from -0.5 to 0.5
- value_projection_matrix: bfloat16 [5120, 2560], P('dp', 'tensor'), may hold values from -0.078125 to 0.078125
- adapter_down_maps: bfloat16 [2, 8, 5120], replicated, may hold values from -0.078125 to 0.078125
- adapter_up_maps: bfloat16 [2, 8, 2560], P(None, None, 'tensor'), may hold values from -1 to 1
- cotangent: bfloat16 [64, 512, 2560], P('dp', None, 'tensor'), may hold values from -6 to 6
- lengths: int32 [64], P('dp'), may hold values from 1 to 512, 16640 in all
- random_signs_down: bfloat16 [2, 8, 5120, 4096], P(None, None, ('dp', 'tensor')), may hold values from -4 to 4
- random_signs_up: bfloat16 [2, 8, 20, 128, 4096], P(None, None, 'tensor', 'dp'), may hold values from -4 to 4
Outputs:
- features: float32 [64, 4096], P('dp', 'tensor')
Inputs may be any that keep to these rules, and one draw needn't show every extreme that they name: `lengths`: positions at or beyond an example's length are padding.
All inputs are finite; a program needn't handle non-finite values. No bound on the sum of `lengths` on one device may be relied on, other than what follows from the above.
Results may differ from a plain program's by a relative error of at most 0.025.
Values may be sent and summed in bfloat16 or wider, within the bound.
A program may use at most 128 MiB of HBM per device.

v0:
```python
import jax
import jax.numpy as jnp
from jax import lax
from jax.sharding import PartitionSpec as P

HEAD_DIM = 128
ADAPTER_RANK = 8
FEAT = 4096


adapter_scale = 2.0
rope_base = 10000.0
norm_eps = 1e-05
masked_score = -1e30


def rope_tables(seq_len, head_width):
    half_width = head_width // 2
    frequency = rope_base ** (-2.0 * jnp.arange(half_width, dtype=jnp.float32) / head_width)
    angles = jnp.arange(seq_len, dtype=jnp.float32)[:, None] * frequency[None, :]
    rotary_cosines = jnp.concatenate([jnp.cos(angles), jnp.cos(angles)], axis=1)
    rotary_sines = jnp.concatenate([jnp.sin(angles), jnp.sin(angles)], axis=1)
    return (rotary_cosines, rotary_sines)


def apply_rotary(tensor_in, rotary_cosines, rotary_sines):
    half_width = tensor_in.shape[-1] // 2
    turned = jnp.concatenate([-tensor_in[..., half_width:], tensor_in[..., :half_width]], axis=-1)
    return tensor_in * rotary_cosines[:, None, :] + turned * rotary_sines[:, None, :]


def unrotate(gradient, rotary_cosines, rotary_sines):
    half_width = gradient.shape[-1] // 2
    scaled = gradient * rotary_sines[:, None, :]
    rotated_back = jnp.concatenate([scaled[..., half_width:], -scaled[..., :half_width]], axis=-1)
    return gradient * rotary_cosines[:, None, :] + rotated_back


def attention_grads(example):
    query_per_head, key_heads, value_per_head, grad_out, seq_length = example
    seq_len = query_per_head.shape[0]
    inv_root = query_per_head.shape[-1] ** (-0.5)
    scores = (
        jnp.einsum("qhc,khc->hqk", query_per_head, key_heads, preferred_element_type=jnp.float32)
        * inv_root
    )
    query_pos = jnp.arange(seq_len, dtype=jnp.int32)[:, None]
    key_pos = jnp.arange(seq_len, dtype=jnp.int32)[None, :]
    allowed = (key_pos <= query_pos) & (key_pos < seq_length)
    scores = jnp.where(allowed[None], scores, masked_score)
    row_max = jnp.max(scores, axis=-1, keepdims=True)
    expon = jnp.exp(scores - row_max)
    attention = expon / jnp.sum(expon, axis=-1, keepdims=True)
    attention_low = attention.astype(jnp.bfloat16)
    grad_values = jnp.einsum(
        "hqk,qhc->khc", attention_low, grad_out, preferred_element_type=jnp.float32
    )
    grad_attention = jnp.einsum(
        "qhc,khc->hqk", grad_out, value_per_head, preferred_element_type=jnp.float32
    )
    inner_sum = jnp.sum(attention * grad_attention, axis=-1, keepdims=True)
    grad_scores = (attention * (grad_attention - inner_sum)).astype(jnp.bfloat16)
    grad_query = (
        jnp.einsum("hqk,khc->qhc", grad_scores, key_heads, preferred_element_type=jnp.float32)
        * inv_root
    )
    return (grad_query, grad_values)


def body(
    hidden,
    query_projection_matrix,
    key_projection_matrix,
    value_projection_matrix,
    adapter_down_maps,
    adapter_up_maps,
    cotangent,
    lengths,
    random_signs_down,
    random_signs_up,
):
    seq_count, seq_len, model_width = hidden.shape
    local_cols = query_projection_matrix.shape[1]
    heads_local = local_cols // HEAD_DIM
    token_matrix = hidden.reshape(seq_count * seq_len, model_width)

    def add_rows(weight_piece):
        return jnp.dot(token_matrix, weight_piece, preferred_element_type=jnp.float32)

    plain_query = add_rows(lax.all_gather(query_projection_matrix, "dp", axis=0, tiled=True))
    base_key = add_rows(lax.all_gather(key_projection_matrix, "dp", axis=0, tiled=True))
    plain_value = add_rows(lax.all_gather(value_projection_matrix, "dp", axis=0, tiled=True))
    rotary_cosines, rotary_sines = rope_tables(seq_len, HEAD_DIM)
    inner_hidden = jnp.einsum(
        "no,wio->nwi", token_matrix, adapter_down_maps, preferred_element_type=jnp.float32
    ).astype(jnp.bfloat16)
    raised_features = jnp.einsum(
        "kdg,dgj->kdj", inner_hidden, adapter_up_maps, preferred_element_type=jnp.float32
    )
    head_layout = (seq_count, seq_len, heads_local, HEAD_DIM)
    query_per_head = apply_rotary(
        (plain_query + adapter_scale * raised_features[:, 0]).reshape(head_layout),
        rotary_cosines,
        rotary_sines,
    ).astype(jnp.bfloat16)
    key_heads = apply_rotary(base_key.reshape(head_layout), rotary_cosines, rotary_sines).astype(
        jnp.bfloat16
    )
    value_per_head = (
        (plain_value + adapter_scale * raised_features[:, 1])
        .astype(jnp.bfloat16)
        .reshape(head_layout)
    )
    valid = jnp.arange(seq_len, dtype=jnp.int32)[None, :] < lengths[:, None]
    masked_out = jnp.where(valid[:, :, None], cotangent, jnp.zeros_like(cotangent)).reshape(
        head_layout
    )
    grad_query, grad_values = lax.map(
        attention_grads, (query_per_head, key_heads, value_per_head, masked_out, lengths)
    )
    grad_query = (
        unrotate(grad_query, rotary_cosines, rotary_sines)
        .astype(jnp.bfloat16)
        .reshape(seq_count, seq_len, local_cols)
    )
    grad_values = grad_values.astype(jnp.bfloat16).reshape(seq_count, seq_len, local_cols)
    per_head_gradient = jnp.stack([grad_query, grad_values], axis=2)
    branch_portion = jnp.einsum(
        "liov,ohv->lioh", per_head_gradient, adapter_up_maps, preferred_element_type=jnp.float32
    )
    adapter_branch = lax.psum(branch_portion, "tensor").astype(jnp.bfloat16)
    middle_seq = inner_hidden.reshape(seq_count, seq_len, 2, ADAPTER_RANK)
    up_map_gradient = adapter_scale * jnp.einsum(
        "esar,esac->earc", middle_seq, per_head_gradient, preferred_element_type=jnp.float32
    )
    parts_dp = lax.axis_size("dp")
    parts_tensor = lax.axis_size("tensor")
    row_block = model_width // (parts_dp * parts_tensor)
    hidden_blocks = hidden.reshape(seq_count, seq_len, parts_dp, parts_tensor, row_block)
    local_column_range = lax.dynamic_index_in_dim(
        hidden_blocks, lax.axis_index("tensor"), axis=3, keepdims=False
    )
    down_map_local = adapter_scale * jnp.einsum(
        "ykzu,ykhc->yhzuc", adapter_branch, local_column_range, preferred_element_type=jnp.float32
    )
    down_map_local = down_map_local.reshape(seq_count, parts_dp, 1, 2 * ADAPTER_RANK * row_block)
    slice_len = HEAD_DIM // parts_dp
    up_blocks = up_map_gradient.reshape(
        seq_count, 2, ADAPTER_RANK, heads_local, parts_dp, slice_len
    )
    up_blocks = up_blocks.transpose(0, 4, 1, 2, 3, 5).reshape(
        seq_count, parts_dp, 1, 2 * ADAPTER_RANK * heads_local * slice_len
    )
    packed = jnp.concatenate([down_map_local, up_blocks], axis=3).astype(jnp.bfloat16)
    routed = lax.all_to_all(packed, "dp", split_axis=1, concat_axis=0, tiled=True)
    gathered = routed.reshape(routed.shape[0], routed.shape[3])
    down_count = down_map_local.shape[3]
    down_table = random_signs_down.reshape(down_count, random_signs_down.shape[-1])
    up_table = random_signs_up.reshape(gathered.shape[1] - down_count, random_signs_up.shape[-1])
    own_rows = lax.psum_scatter(
        (
            jnp.dot(gathered[:, :down_count], down_table, preferred_element_type=jnp.float32)
            + jnp.dot(gathered[:, down_count:], up_table, preferred_element_type=jnp.float32)
        ).astype(jnp.bfloat16),
        "dp",
        scatter_dimension=0,
        tiled=True,
    )
    features_local = lax.psum_scatter(own_rows, "tensor", scatter_dimension=1, tiled=True).astype(
        jnp.float32
    )
    squares = lax.psum(jnp.sum(features_local * features_local, axis=1), "tensor")
    return features_local * lax.rsqrt(squares / FEAT + norm_eps)[:, None]


def solution(mesh):
    return jax.shard_map(
        body,
        mesh=mesh,
        in_specs=(
            P("dp", None, None),
            P("dp", "tensor"),
            P("dp", "tensor"),
            P("dp", "tensor"),
            P(),
            P(None, None, "tensor"),
            P("dp", None, "tensor"),
            P("dp"),
            P(None, None, ("dp", "tensor"), None),
            P(None, None, "tensor", "dp", None),
        ),
        out_specs=P("dp", "tensor"),
        check_vma=False,
    )
```

profile of v0, /device:TPU:1, one launch (start us, length us, event | category | flops | bytes accessed | tf_op | source)
XLA Modules:
  0.0 960.9 jit_solution(16384661594422788543)
XLA Ops:
  10.4 13.8 %copy.51 = bf16[2,512,5120]{1,2,0:T(8,128)(2,1)} copy(bf16[2,512,5120]{2,1,0:T(8,128)(2,1)} %param.12) | data formatting | bytes 20971520 | tf_op args[0]
  26.1 6.8 convolution_convert_fusion
  33.5 3.2 convolution_bitcast_fusion
  36.7 117.4 %all-gather.6.cloned.1.call-done = bf16[5120,640]{1,0:T(8,128)(2,1)} async-done(((bf16[160,640]{1,0:T(8,128)(2,1)}), bf16[5120,640]{1,0:T(8,128)(2,1)}) %all-gather.6.cloned.1.call-update) | async-done | bytes 6553616 | tf_op jit(solution)/shard_map/all_gather | solution.py:90
  154.2 13.3 %fusion.46 = f32[1024,640]{1,0:T(8,128)S(1)} fusion(f32[1024,2,640]{2,0,1:T(8,128)} %convolution_bitcast_fusion, bf16[1024,5120]{1,0:T(8,128)(2,1)} %bitcast.136, bf16[5120,640]{1,0:T(8,128)(2,1)} %all-gather.6.cloned.1.call-done), kind=kOutput, calls=%fused_computation.52 | convolution fusion | flops 6712197120 | bytes 22282240 | tf_op jit(solution)/shard_map/dot_general | solution.py:88
  167.5 2.3 reshape.164
  169.8 3.3 copy.54
  173.1 145.5 %all-gather.4.cloned.1.call-done = bf16[5120,640]{1,0:T(8,128)(2,1)} async-done(((bf16[160,640]{1,0:T(8,128)(2,1)}), bf16[5120,640]{1,0:T(8,128)(2,1)}) %all-gather.4.cloned.1.call-update) | async-done | bytes 6553616 | tf_op jit(solution)/shard_map/all_gather | solution.py:91
  318.6 9.6 copy.52
  330.1 11.9 %fusion.39 = f32[2,512,5,128]{1,3,2,0:T(8,128)S(1)} fusion(bf16[5,128,5120,1]{2,1,0,3:T(8,128)(2,1)} %bitcast.140, bf16[2,512,5120]{2,1,0:T(8,128)(2,1)} %param.12), kind=kOutput, calls=%fused_computation.42 | convolution fusion | flops 6710886400 | bytes 19660800 | tf_op jit(solution)/shard_map/dot_general | solution.py:88
  345.2 137.9 %all-gather.8.cloned.1.call-done = bf16[5120,640]{1,0:T(8,128)(2,1)} async-done(((bf16[160,640]{1,0:T(8,128)(2,1)}), bf16[5120,640]{1,0:T(8,128)(2,1)}) %all-gather.8.cloned.1.call-update) | async-done | bytes 6553616 | tf_op jit(solution)/shard_map/all_gather | solution.py:92
  483.1 14.2 %fusion.44 = bf16[1024,640]{1,0:T(8,128)(2,1)} fusion(f32[1024,2,640]{2,0,1:T(8,128)} %convolution_bitcast_fusion, bf16[1024,5120]{1,0:T(8,128)(2,1)} %bitcast.137, bf16[5120,640]{1,0:T(8,128)(2,1)} %all-gather.8.cloned.1.call-done), kind=kOutput, calls=%fused_computation.49 | convolution fusion | flops 6712852480 | bytes 20971520 | tf_op jit(solution)/shard_map/dot_general | solution.py:88
  497.3 4.1 reshape.160
  501.4 3.1 copy.62
  504.4 5.5 fusion.50
  509.9 22.3 %while.12 = (s32[]{:T(128)}, f32[2,512,5,128]{1,3,2,0:T(8,128)}, bf16[2,512,5,128]{1,3,2,0:T(8,128)(2,1)}, bf16[2,512,5,128]{1,3,2,0:T(8,128)(2,1)}, s32[2]{0:T(...) while((s32[]{:T(128)}, f32[2,512,5,128]{1,3,2,0:T(8,128)}, ...), condition=%wide.region_4.5_spmd, body=%wide.region_0.4_spmd.sunk | while | flops 1362688512 | bytes 75326712 | solution.py:118
  509.9 2.2 fusion.110
  513.5 2.5 fusion.112
  518.9 2.2 fusion.113
  521.1 2.2 fusion.110
  524.6 2.5 fusion.112
  530.0 2.2 fusion.113
  534.6 2.5 fusion.51
  542.1 34.5 %psum.14 = bf16[2,512,2,8]{1,3,2,0:T(8,128)(2,1)S(1)} all-reduce(f32[2,512,2,8]{1,3,2,0:T(8,128)S(1)} %fusion.67), channel_id=1, replica_groups=mesh['dp'=32,'tensor'=4] {'tensor'}, use_global_device_ids=true, to_apply=%region_5.6 | all-reduce | flops 16384 | bytes 98304 | tf_op jit(solution)/shard_map/psum | solution.py:131
  576.6 3.3 fusion.63
  582.4 6.6 all-to-all-start
  589.1 3.5 reshape.153
  592.6 3.8 all-to-all-done
  596.6 3.6 fusion.71
  602.9 286.6 %all-reduce.3.cloned.1.call-done = bf16[64,4096]{1,0:T(8,128)(2,1)} async-done(((bf16[64,4096]{1,0:T(8,128)(2,1)}), bf16[64,4096]{1,0:T(8,128)(2,1)}) %all-reduce.3.cloned.1.call-update) | async-done | bytes 524304
  891.8 53.3 %reduce-scatter.4.cloned.1.call-done = bf16[1024,2]{1,0:T(8,128)(2,1)} async-done(((bf16[4096,2]{1,0:T(8,128)(2,1)}), bf16[1024,2]{1,0:T(8,128)(2,1)}) %reduce-scatter.4.cloned.1.call-update) | async-done | bytes 4112
  946.3 7.4 psum.15
  (97 shorter events, 36.0 us)
Async XLA Ops:
  6.5 19.5 %copy-start = (bf16[2,8,5120]{2,1,0:T(8,128)(2,1)S(1)}, bf16[2,8,5120]{2,1,0:T(8,128)(2,1)}, u32[]{:S(2)}) copy-start(bf16[2,8,5120]{2,1,0:T(8,128)(2,1)} %param.16) | copy-start | bytes 491524
  6.5 147.6 %all-gather.6.cloned.1.call-start = ((), (), s32[]{:S(2)}) async-start(), calls=%async_computation.3 | async-start | bytes 6758400 | tf_op jit(solution)/shard_map/all_gather | solution.py:90
  7.3 311.3 %all-gather.4.cloned.1.call-start = ((), (), s32[]{:S(2)}) async-start(), calls=%async_computation.2 | async-start | bytes 6758400 | tf_op jit(solution)/shard_map/all_gather | solution.py:91
  8.0 475.1 %all-gather.8.cloned.1.call-start = ((), (), s32[]{:S(2)}) async-start(), calls=%async_computation.4 | async-start | bytes 6758400 | tf_op jit(solution)/shard_map/all_gather | solution.py:92
  10.4 14.5 %copy-start.16 = (s32[2]{0:T(128)S(1)}, s32[2]{0:T(128)}, u32[]{:S(2)}) copy-start(s32[2]{0:T(128)} %param.19) | copy-start | bytes 28
  26.1 7.5 copy-start.14
  32.9 0.6 copy-start.12
  341.9 1.5 copy-start.3
  501.4 3.1 copy-start.4
  513.5 2.6 copy-start.5
  513.5 2.6 copy-start.11
  516.1 1.3 copy-start.8
  517.1 1.2 copy-start.6
  517.4 1.5 copy-start.2
  524.6 2.6 copy-start.5
  524.6 2.6 copy-start.11
  527.2 1.3 copy-start.8
  528.2 1.2 copy-start.6
  528.5 1.5 copy-start.2
  537.1 1.5 copy-start.7
  537.1 2.9 copy-start.15
  538.6 1.4 copy-start.9
  542.1 38.1 %copy-start.10 = (bf16[2,512,1,640]{3,1,2,0:T(8,128)(2,1)S(1)}, bf16[2,512,1,640]{3,1,2,0:T(8,128)(2,1)}, u32[]{:S(2)}) copy-start(bf16[2,512,1,640]{3,1,2,0:T(8,128)(2,1)} %copy.64) | copy-start | bytes 3932164
  542.1 38.1 %copy-start.13 = (bf16[1024,2,8]{0,2,1:T(8,128)(2,1)S(1)}, bf16[1024,2,8]{0,2,1:T(8,128)(2,1)}, u32[]{:S(2)}) copy-start(bf16[1024,2,8]{0,2,1:T(8,128)(2,1)} %copy-done.12) | copy-start | bytes 98308
  582.4 14.1 %all-to-all-start = ((bf16[2,32,1,960]{3,0,2,1:T(2,128)(2,1)}), bf16[2,32,1,960]{3,0,2,1:T(2,128)(2,1)S(1)}, u32[]{:S(2)}, u32[]{:S(2)}) async-start(bf16[2,32,1,960]{3,0,2,1:T(2,128)(2,1)} %pad_maximum_fusion.11), calls=%async_computation | async-start | bytes 262144 | tf_op jit(solution)/shard_map/all_to_all | solution.py:155
  589.1 300.5 %all-reduce.3.cloned.1.call-start = ((), (), s32[]{:S(2)}) async-start(), calls=%async_computation.6 | async-start | bytes 1048576
  596.5 357.8 %copy-start.1 = (bf16[2,8,5120]{2,1,0:T(8,128)(2,1)S(1)}, bf16[2,8,5120]{2,1,0:T(8,128)(2,1)}, u32[]{:S(2)}) copy-start(bf16[2,8,5120]{2,1,0:T(8,128)(2,1)} %param.16) | copy-start | bytes 491524
  600.1 1.6 copy-start.17
  601.6 343.4 %reduce-scatter.4.cloned.1.call-start = ((), (), s32[]{:S(2)}) async-start(), calls=%async_computation.5 | async-start | bytes 1310720
Sparse Core Ops, SparseCore 0:
  9.0 145.1 all-gather.5
  155.8 162.7 all-gather.3
  320.2 162.8 all-gather.7
  601.8 287.7 all-reduce.2
  892.0 53.0 reduce-scatter.3
where the time goes:
time: 962 us; the launch traced here: 961 us
  waiting for transfers between devices  747 us (78%)
  matrix products  72.7 us (8%)
  local copies, waits for them, and re-layouts  54.7 us (6%)
  blocking collectives  41.9 us (4%)
  other arithmetic  24.1 us (3%)
  between operations  14.1 us (1%)
    unnamed x7, waiting for transfers between devices  342 us
    all_gather x1, waiting for transfers between devices, body(): lax.all_gather(key_projection_matrix, 'dp', axis=0, tiled=True)  145 us
    all_gather x1, waiting for transfers between devices, body(): lax.all_gather(value_projection_matrix, 'dp', axis=0, tiled=True)  138 us
    all_gather x1, waiting for transfers between devices, body(): lax.all_gather(query_projection_matrix, 'dp', axis=0, tiled=True)  117 us
    dot_general x3, matrix products, add_rows(): jnp.dot(token_matrix, weight_piece, preferred_element_type=jnp.float32)  39.3 us
    psum x1, blocking collectives, body(): adapter_branch = lax.psum(branch_portion, 'tensor').astype(jnp.bfloat16)  34.5 us
    unnamed x32, local copies, waits for them, and re-layouts  21.5 us
  transfers between devices with their start and end apart: 6, of which 6 were waited for; matrix products, arithmetic and copies ran while one was open for 8% of the time, Pallas kernels for 0%

commit v1 on v0

--- a/solution.py
+++ b/solution.py
@@ -87,9 +87,18 @@
     def add_rows(weight_piece):
         return jnp.dot(token_matrix, weight_piece, preferred_element_type=jnp.float32)
 
-    plain_query = add_rows(lax.all_gather(query_projection_matrix, "dp", axis=0, tiled=True))
-    base_key = add_rows(lax.all_gather(key_projection_matrix, "dp", axis=0, tiled=True))
-    plain_value = add_rows(lax.all_gather(value_projection_matrix, "dp", axis=0, tiled=True))
+    parts_dp = lax.axis_size("dp")
+    local_rows = jnp.concatenate(
+        [query_projection_matrix, key_projection_matrix, value_projection_matrix], axis=1
+    )
+    copies = jnp.broadcast_to(local_rows[None], (parts_dp,) + local_rows.shape)
+    all_rows = lax.all_to_all(copies, "dp", 0, 0, tiled=True).reshape(
+        parts_dp * local_rows.shape[0], local_rows.shape[1]
+    )
+    projected = add_rows(all_rows)
+    plain_query = projected[:, :local_cols]
+    base_key = projected[:, local_cols : 2 * local_cols]
+    plain_value = projected[:, 2 * local_cols :]
     rotary_cosines, rotary_sines = rope_tables(seq_len, HEAD_DIM)
     inner_hidden = jnp.einsum(
         "no,wio->nwi", token_matrix, adapter_down_maps, preferred_element_type=jnp.float32
@@ -133,7 +142,6 @@
     up_map_gradient = adapter_scale * jnp.einsum(
         "esar,esac->earc", middle_seq, per_head_gradient, preferred_element_type=jnp.float32
     )
-    parts_dp = lax.axis_size("dp")
     parts_tensor = lax.axis_size("tensor")
     row_block = model_width // (parts_dp * parts_tensor)
     hidden_blocks = hidden.reshape(seq_count, seq_len, parts_dp, parts_tensor, row_block)
@@ -157,18 +165,20 @@
     down_count = down_map_local.shape[3]
     down_table = random_signs_down.reshape(down_count, random_signs_down.shape[-1])
     up_table = random_signs_up.reshape(gathered.shape[1] - down_count, random_signs_up.shape[-1])
-    own_rows = lax.psum_scatter(
-        (
-            jnp.dot(gathered[:, :down_count], down_table, preferred_element_type=jnp.float32)
-            + jnp.dot(gathered[:, down_count:], up_table, preferred_element_type=jnp.float32)
-        ).astype(jnp.bfloat16),
-        "dp",
-        scatter_dimension=0,
-        tiled=True,
-    )
-    features_local = lax.psum_scatter(own_rows, "tensor", scatter_dimension=1, tiled=True).astype(
-        jnp.float32
-    )
+    partial = (
+        jnp.dot(gathered[:, :down_count], down_table, preferred_element_type=jnp.float32)
+        + jnp.dot(gathered[:, down_count:], up_table, preferred_element_type=jnp.float32)
+    ).astype(jnp.bfloat16)
+    own_count = partial.shape[0] // parts_dp
+    to_owner = lax.all_to_all(
+        partial.reshape(parts_dp, own_count, partial.shape[1]), "dp", 0, 0, tiled=True
+    )
+    own_rows = jnp.sum(to_owner.astype(jnp.float32), axis=0)
+    feat_block = own_rows.shape[1] // parts_tensor
+    to_block = lax.all_to_all(
+        own_rows.reshape(own_count, parts_tensor, feat_block), "tensor", 1, 1, tiled=True
+    )
+    features_local = jnp.sum(to_block, axis=1)
     squares = lax.psum(jnp.sum(features_local * features_local, axis=1), "tensor")
     return features_local * lax.rsqrt(squares / FEAT + norm_eps)[:, None]
 

time: 962 us -> 528 us (0.55)
  waiting for transfers between devices: 747 us -> 292 us
  starting transfers between devices: 6.8 us -> 36.4 us
  between operations: 14.1 us -> 0.26 us
  matrix products: 72.7 us -> 61.1 us
    all_gather x3 -> x0, waiting for transfers between devices: 401 us -> none  [the longest x1 145 us: body(): lax.all_gather(key_projection_matrix, 'dp', axis=0, tiled=True)]
    unnamed x7 -> x0, waiting for transfers between devices: 342 us -> none
    all_to_all x0 -> x1, waiting for transfers between devices: none -> 288 us  [body(): lax.all_to_all(copies, 'dp', 0, 0, tiled=True)]
    all_to_all x0 -> x2, blocking collectives: none -> 25.1 us  [the longest x1 12.8 us: body(): lax.all_to_all(partial.reshape(parts_dp, own_count, partial.shape[1]), 'd...]
    all_to_all x1, starting transfers between devices: 6.64 us -> 26.9 us  [body(): lax.all_to_all(packed, 'dp', split_axis=1, concat_axis=0, tiled=True)]
    psum x1, blocking collectives: 34.5 us -> 17 us  [body(): adapter_branch = lax.psum(branch_portion, 'tensor').astype(jnp.bfloat16)]
    dot_general x3 -> x1, matrix products: 39.3 us -> 28.5 us  [add_rows(): jnp.dot(token_matrix, weight_piece, preferred_element_type=jnp.float32)]
    unnamed x32 -> x26, local copies, waits for them, and re-layouts: 21.5 us -> 15.1 us
  transfers between devices with their start and end apart: 6 -> 2, of which waited for: 6 -> 2; matrix products, arithmetic and copies ran while one was open for 8% -> 6% of each run, Pallas kernels for 0% -> 0%
where the time goes in v1:
time: 528 us; the launch traced here: 527 us
  waiting for transfers between devices  292 us (55%)
  matrix products  61.1 us (12%)
  local copies, waits for them, and re-layouts  56.1 us (11%)
  blocking collectives  49.5 us (9%)
  starting transfers between devices  36.4 us (7%)
  other arithmetic  31.3 us (6%)
    all_to_all x1, waiting for transfers between devices, body(): lax.all_to_all(copies, 'dp', 0, 0, tiled=True)  288 us
    dot_general x1, matrix products, add_rows(): jnp.dot(token_matrix, weight_piece, preferred_element_type=jnp.float32)  28.5 us
    all_to_all x1, starting transfers between devices, body(): lax.all_to_all(packed, 'dp', split_axis=1, concat_axis=0, tiled=True)  26.9 us
    psum x1, blocking collectives, body(): adapter_branch = lax.psum(branch_portion, 'tensor').astype(jnp.bfloat16)  17 us
    unnamed x26, local copies, waits for them, and re-layouts  15.1 us
    all_to_all x1, blocking collectives, body(): lax.all_to_all(partial.reshape(parts_dp, own_count, partial.shape[1]), 'd...  12.8 us
    all_to_all x1, blocking collectives, body(): lax.all_to_all(own_rows.reshape(own_count, parts_tensor, feat_block), 'te...  12.3 us
  transfers between devices with their start and end apart: 2, of which 2 were waited for; matrix products, arithmetic and copies ran while one was open for 6% of the time, Pallas kernels for 0%

profile of v1, /device:TPU:1, one launch (start us, length us, event | category | flops | bytes accessed | tf_op | source)
XLA Modules:
  0.0 526.6 jit_solution(15790345777017268818)
XLA Ops:
  1.2 6.9 %broadcast_in_dim.30 = bf16[32,160,1920]{2,1,0:T(8,128)(2,1)} broadcast(bf16[160,1920]{1,0:T(8,128)(2,1)S(1)} %pad_maximum_fusion.9), dimensions={1,2} | broadcast | bytes 20275200 | tf_op jit(solution)/shard_map/broadcast_in_dim | solution.py:94
  8.1 9.5 %all-to-all-start = ((bf16[32,160,1920]{2,1,0:T(8,128)(2,1)}), bf16[32,160,1920]{2,1,0:T(8,128)(2,1)}, u32[]{:S(2)}, u32[]{:S(2)}) async-start(bf16[32,160,1920]{2,1,0:T(8,128)(2,1)} %broadcast_in_dim.30), calls=%async_computation | async-start | bytes 39321600 | tf_op jit(solution)/shard_map/all_to_all | solution.py:95
  18.3 13.8 %copy.58 = bf16[2,512,5120]{1,2,0:T(8,128)(2,1)} copy(bf16[2,512,5120]{2,1,0:T(8,128)(2,1)} %param.12) | data formatting | bytes 20971520 | tf_op args[0]
  33.9 6.8 %convolution_convert_fusion = bf16[1024,2,8]{0,2,1:T(8,128)(2,1)S(1)} fusion(bf16[1024,5120,1]{1,0,2:T(8,128)(2,1)} %bitcast.130, bf16[2,8,5120]{2,1,0:T(8,128)(2,1)S(1)} %copy-done), kind=kOutput, calls=%fused_computation.78 | convolution fusion | flops 167788544 | bytes 10682368 | tf_op jit(solution)/shard_map/no,wio->nwi/dot_general | solution.py:103
  41.4 3.2 convolution_bitcast_fusion.1
  44.6 287.9 %all-to-all-done = bf16[32,160,1920]{2,1,0:T(8,128)(2,1)} async-done(((bf16[32,160,1920]{2,1,0:T(8,128)(2,1)}), bf16[32,160,1920]{2,1,0:T(8,128)(2,1)}, u32[]{:S(2)}, u32[]{:S(2)}) %all-to-all-start) | async-done | bytes 19660832 | tf_op jit(solution)/shard_map/all_to_all | solution.py:95
  332.5 28.5 %convolution_bitcast_fusion = f32[1024,1920]{0,1:T(8,128)} fusion(bf16[5120,1920]{1,0:T(8,128)(2,1)} %bitcast.13, bf16[1024,5120]{1,0:T(8,128)(2,1)} %bitcast.131), kind=kOutput, calls=%fused_computation.44 | convolution fusion | flops 20132659200 | bytes 38010880 | tf_op jit(solution)/shard_map/dot_general | solution.py:88
  361.1 8.7 %fusion.42 = (bf16[1024,640]{0,1:T(8,128)(2,1)}, f32[1024,640]{0,1:T(8,128)}, f32[1024,640]{0,1:T(8,128)}) fusion(f32[1024,2,640]{0,2,1:T(8,128)} %convolution_bitcast_fusion.1, f32[1024,1920]{0,1:T(8,128)} %convolution_bitcast_fusion), kind=kLoop, calls=%fused_computation.48 | loop fusion | flops 3276800 | bytes 19660800 | tf_op jit(solution)/shard_map/convert_element_type | solution.py:120
  369.7 3.7 reshape.156
  375.4 4.8 reshape.157
  380.2 3.8 copy.63
  384.0 4.4 reshape.159
  388.4 4.3 copy.70
  392.6 3.4 slice_negate_fusion.1
  396.0 2.7 fusion.48
  398.7 22.4 %while.12 = (s32[]{:T(128)}, f32[2,512,5,128]{1,3,2,0:T(8,128)}, bf16[2,512,5,128]{1,3,2,0:T(8,128)(2,1)}, bf16[2,512,5,128]{1,3,2,0:T(8,128)(2,1)}, s32[2]{0:T(...) while((s32[]{:T(128)}, f32[2,512,5,128]{1,3,2,0:T(8,128)}, ...), condition=%wide.region_4.5_spmd, body=%wide.region_0.4_spmd.sunk | while | flops 1362688512 | bytes 75326712 | solution.py:127
  398.7 2.2 fusion.104
  402.4 2.5 fusion.106
  407.7 2.2 fusion.107
  409.9 2.2 fusion.104
  413.6 2.5 fusion.106
  418.9 2.2 fusion.107
  423.5 2.5 fusion.49
  431.0 17.0 %psum.14 = bf16[2,512,2,8]{1,3,2,0:T(8,128)(2,1)S(1)} all-reduce(f32[2,512,2,8]{1,3,2,0:T(8,128)S(1)} %fusion.65), channel_id=1, replica_groups=mesh['dp'=32,'tensor'=4] {'tensor'}, use_global_device_ids=true, to_apply=%region_5.6 | all-reduce | flops 16384 | bytes 98304 | tf_op jit(solution)/shard_map/psum | solution.py:140
  448.0 3.3 fusion.61
  453.8 26.9 %all-to-all-start.1 = ((bf16[2,32,1,960]{3,0,2,1:T(2,128)(2,1)}), bf16[2,32,1,960]{3,0,2,1:T(2,128)(2,1)S(1)}, u32[]{:S(2)}, u32[]{:S(2)}) async-start(bf16[2,32,1,960]{3,0,2,1:T(2,128)(2,1)} %pad_maximum_fusion.12), calls=%async_computation.1 | async-start | bytes 262144 | tf_op jit(solution)/shard_map/all_to_all | solution.py:163
  480.8 3.5 reshape.164
  484.3 3.9 all-to-all-done.1
  488.3 3.6 fusion.69
  492.9 12.8 %all_to_all.30 = bf16[32,2,4096]{2,1,0:T(2,128)(2,1)S(1)} all-to-all(bf16[32,2,4096]{2,1,0:T(2,128)(2,1)S(1)} %reshape.165), channel_id=1, replica_groups=mesh['dp'=32,'tensor'=4] {'dp'}, dimensions={0} | all-to-all | bytes 1048576 | tf_op jit(solution)/shard_map/all_to_all | solution.py:173
  506.1 12.3 %all_to_all.31 = f32[2,4,1024]{2,0,1:T(2,128)S(1)} all-to-all(f32[2,4,1024]{2,0,1:T(2,128)S(1)} %bitcast.141), channel_id=1, replica_groups=mesh['dp'=32,'tensor'=4] {'tensor'}, dimensions={1} | all-to-all | bytes 65536 | tf_op jit(solution)/shard_map/all_to_all | solution.py:178
  518.6 7.3 %psum.15 = f32[2]{0:T(128)S(1)} all-reduce(f32[2]{0:T(128)S(1)} %multiply_reduce_fusion.1), channel_id=1, replica_groups=mesh['dp'=32,'tensor'=4] {'tensor'}, use_global_device_ids=true, to_apply=%region_9.10 | all-reduce | flops 2 | bytes 16 | tf_op jit(solution)/shard_map/psum | solution.py:182
  (84 shorter events, 27.0 us)
Async XLA Ops:
  0.0 33.9 %copy-start = (bf16[2,8,5120]{2,1,0:T(8,128)(2,1)S(1)}, bf16[2,8,5120]{2,1,0:T(8,128)(2,1)}, u32[]{:S(2)}) copy-start(bf16[2,8,5120]{2,1,0:T(8,128)(2,1)} %param.16) | copy-start | bytes 491524
  8.1 9.5 %copy-start.4 = (bf16[2,512,640]{2,1,0:T(8,128)(2,1)S(1)}, bf16[2,512,640]{2,1,0:T(8,128)(2,1)}, u32[]{:S(2)}) copy-start(bf16[2,512,640]{2,1,0:T(8,128)(2,1)} %param.18) | copy-start | bytes 3932164
  8.1 324.4 %all-to-all-start = ((bf16[32,160,1920]{2,1,0:T(8,128)(2,1)}), bf16[32,160,1920]{2,1,0:T(8,128)(2,1)}, u32[]{:S(2)}, u32[]{:S(2)}) async-start(bf16[32,160,1920]{2,1,0:T(8,128)(2,1)} %broadcast_in_dim.30), calls=%async_computation | async-start | bytes 39321600 | tf_op jit(solution)/shard_map/all_to_all | solution.py:95
  18.2 14.4 %copy-start.16 = (s32[2]{0:T(128)S(1)}, s32[2]{0:T(128)}, u32[]{:S(2)}) copy-start(s32[2]{0:T(128)} %param.19) | copy-start | bytes 28
  33.9 7.4 %copy-start.14 = (bf16[2,8,640]{2,1,0:T(8,128)(2,1)S(1)}, bf16[2,8,640]{2,1,0:T(8,128)(2,1)}, u32[]{:S(2)}) copy-start(bf16[2,8,640]{2,1,0:T(8,128)(2,1)} %param.17) | copy-start | bytes 61444
  40.7 0.6 copy-start.12
  392.6 3.4 copy-start.2
  402.4 2.6 copy-start.5
  402.4 2.6 copy-start.11
  404.9 1.3 copy-start.8
  405.9 1.2 copy-start.6
  406.2 1.5 copy-start.3
  413.5 2.6 copy-start.5
  413.5 2.6 copy-start.11
  416.1 1.3 copy-start.8
  417.1 1.2 copy-start.6
  417.4 1.5 copy-start.3
  426.0 1.5 copy-start.7
  426.0 2.9 copy-start.15
  427.4 1.5 copy-start.9
  431.0 20.7 %copy-start.10 = (bf16[2,512,1,640]{3,1,2,0:T(8,128)(2,1)S(1)}, bf16[2,512,1,640]{3,1,2,0:T(8,128)(2,1)}, u32[]{:S(2)}) copy-start(bf16[2,512,1,640]{3,1,2,0:T(8,128)(2,1)} %copy.72) | copy-start | bytes 3932164
  431.0 20.7 %copy-start.13 = (bf16[1024,2,8]{0,2,1:T(8,128)(2,1)S(1)}, bf16[1024,2,8]{0,2,1:T(8,128)(2,1)}, u32[]{:S(2)}) copy-start(bf16[1024,2,8]{0,2,1:T(8,128)(2,1)} %copy-done.12) | copy-start | bytes 98308
  453.8 34.4 %all-to-all-start.1 = ((bf16[2,32,1,960]{3,0,2,1:T(2,128)(2,1)}), bf16[2,32,1,960]{3,0,2,1:T(2,128)(2,1)S(1)}, u32[]{:S(2)}, u32[]{:S(2)}) async-start(bf16[2,32,1,960]{3,0,2,1:T(2,128)(2,1)} %pad_maximum_fusion.12), calls=%async_computation.1 | async-start | bytes 262144 | tf_op jit(solution)/shard_map/all_to_all | solution.py:163
  488.3 38.3 %copy-start.1 = (bf16[2,8,5120]{2,1,0:T(8,128)(2,1)S(1)}, bf16[2,8,5120]{2,1,0:T(8,128)(2,1)}, u32[]{:S(2)}) copy-start(bf16[2,8,5120]{2,1,0:T(8,128)(2,1)} %param.16) | copy-start | bytes 491524

commit v2 on v1

--- a/solution.py
+++ b/solution.py
@@ -91,10 +91,7 @@
     local_rows = jnp.concatenate(
         [query_projection_matrix, key_projection_matrix, value_projection_matrix], axis=1
     )
-    copies = jnp.broadcast_to(local_rows[None], (parts_dp,) + local_rows.shape)
-    all_rows = lax.all_to_all(copies, "dp", 0, 0, tiled=True).reshape(
-        parts_dp * local_rows.shape[0], local_rows.shape[1]
-    )
+    all_rows = lax.all_gather(local_rows, "dp", axis=0, tiled=True)
     projected = add_rows(all_rows)
     plain_query = projected[:, :local_cols]
     base_key = projected[:, local_cols : 2 * local_cols]
@@ -175,11 +172,11 @@
     )
     own_rows = jnp.sum(to_owner.astype(jnp.float32), axis=0)
     feat_block = own_rows.shape[1] // parts_tensor
-    to_block = lax.all_to_all(
-        own_rows.reshape(own_count, parts_tensor, feat_block), "tensor", 1, 1, tiled=True
-    )
-    features_local = jnp.sum(to_block, axis=1)
-    squares = lax.psum(jnp.sum(features_local * features_local, axis=1), "tensor")
+    full_rows = lax.psum(own_rows, "tensor")
+    squares = jnp.sum(full_rows * full_rows, axis=1)
+    features_local = lax.dynamic_slice_in_dim(
+        full_rows, lax.axis_index("tensor") * feat_block, feat_block, axis=1
+    )
     return features_local * lax.rsqrt(squares / FEAT + norm_eps)[:, None]
 
 

time: 528 us -> 399 us (0.76)
  waiting for transfers between devices: 292 us -> 210 us
  starting transfers between devices: 36.4 us -> 7.73 us
  blocking collectives: 49.5 us -> 31.4 us
  between operations: 0.26 us -> 13.7 us
  local copies, waits for them, and re-layouts: 56.1 us -> 49.5 us
    all_to_all x1, waiting for transfers between devices: 288 us -> 9.23 us  [body(): lax.all_to_all(partial.reshape(parts_dp, own_count, partial.shape[1]), 'd...]
    all_gather x0 -> x1, waiting for transfers between devices: none -> 197 us  [body(): all_rows = lax.all_gather(local_rows, 'dp', axis=0, tiled=True)]
    all_to_all x2 -> x0, blocking collectives: 25.1 us -> none  [the longest x1 12.8 us: body(): lax.all_to_all(partial.reshape(parts_dp, own_count, partial.shape[1]), 'd...]
    all_to_all x1, starting transfers between devices: 26.9 us -> 3.84 us  [body(): lax.all_to_all(packed, 'dp', split_axis=1, concat_axis=0, tiled=True)]
    psum x1, blocking collectives: 7.29 us -> 17.3 us  [body(): full_rows = lax.psum(own_rows, 'tensor')]
    broadcast_in_dim x1 -> x0, local copies, waits for them, and re-layouts: 6.87 us -> none  [body(): copies = jnp.broadcast_to(local_rows[None], (parts_dp,) + local_rows.shape)]
    all_to_all x1, starting transfers between devices: 9.46 us -> 3.89 us  [body(): lax.all_to_all(partial.reshape(parts_dp, own_count, partial.shape[1]), 'd...]
    unnamed x26 -> x24, local copies, waits for them, and re-layouts: 15.1 us -> 15.9 us
  transfers between devices with their start and end apart: 2 -> 3, of which waited for: 2 -> 3; matrix products, arithmetic and copies ran while one was open for 6% -> 8% of each run, Pallas kernels for 0% -> 0%
where the time goes in v2:
time: 399 us; the launch traced here: 398 us
  waiting for transfers between devices  210 us (53%)
  matrix products  57.6 us (14%)
  local copies, waits for them, and re-layouts  49.5 us (12%)
  blocking collectives  31.4 us (8%)
  other arithmetic  27.9 us (7%)
  between operations  13.7 us (3%)
  starting transfers between devices  7.73 us (2%)
    all_gather x1, waiting for transfers between devices, body(): all_rows = lax.all_gather(local_rows, 'dp', axis=0, tiled=True)  197 us
    dot_general x1, matrix products, add_rows(): jnp.dot(token_matrix, weight_piece, preferred_element_type=jnp.float32)  28.6 us
    psum x1, blocking collectives, body(): full_rows = lax.psum(own_rows, 'tensor')  17.3 us
    unnamed x24, local copies, waits for them, and re-layouts  15.9 us
    psum x1, blocking collectives, body(): adapter_branch = lax.psum(branch_portion, 'tensor').astype(jnp.bfloat16)  14.2 us
    all_to_all x1, waiting for transfers between devices, body(): lax.all_to_all(partial.reshape(parts_dp, own_count, partial.shape[1]), 'd...  9.23 us
    convert_element_type x1, other arithmetic, body(): value_per_head = (plain_value + adapter_scale * raised_features[:, 1]).as...  9.05 us
  transfers between devices with their start and end apart: 3, of which 3 were waited for; matrix products, arithmetic and copies ran while one was open for 8% of the time, Pallas kernels for 0%

profile of v2, /device:TPU:1, one launch (start us, length us, event | category | flops | bytes accessed | tf_op | source)
XLA Modules:
  0.0 397.9 jit_solution(12971542466677714092)
XLA Ops:
  6.5 2.1 pad_maximum_fusion.9
  9.4 13.9 %copy.58 = bf16[2,512,5120]{1,2,0:T(8,128)(2,1)} copy(bf16[2,512,5120]{2,1,0:T(8,128)(2,1)} %param.12) | data formatting | bytes 20971520 | tf_op args[0]
  24.0 1.2 broadcast_select_fusion
  25.1 6.8 %convolution_convert_fusion = bf16[1024,2,8]{0,2,1:T(8,128)(2,1)S(1)} fusion(bf16[1024,5120,1]{1,0,2:T(8,128)(2,1)} %bitcast.128, bf16[2,8,5120]{2,1,0:T(8,128)(2,1)S(1)} %copy-done), kind=kOutput, calls=%fused_computation.78 | convolution fusion | flops 167788544 | bytes 10682368 | tf_op jit(solution)/shard_map/no,wio->nwi/dot_general | solution.py:100
  32.5 3.2 convolution_bitcast_fusion.1
  35.7 196.8 %all-gather.2.cloned.1.call-done = bf16[5120,1920]{1,0:T(8,128)(2,1)} async-done(((bf16[160,1920]{1,0:T(8,128)(2,1)}), bf16[5120,1920]{1,0:T(8,128)(2,1)}) %all-gather.2.cloned.1.call-update) | async-done | bytes 19660816 | tf_op jit(solution)/shard_map/all_gather | solution.py:94
  232.5 28.6 %convolution_bitcast_fusion = f32[1024,1920]{0,1:T(8,128)} fusion(bf16[5120,1920]{1,0:T(8,128)(2,1)} %all-gather.2.cloned.1.call-done, bf16[1024,5120]{1,0:T(8,128)(2,1)} %bitcast.129), kind=kOutput, calls=%fused_computation.44 | convolution fusion | flops 20132659200 | bytes 38010880 | tf_op jit(solution)/shard_map/dot_general | solution.py:88
  261.1 9.0 %fusion.42 = (bf16[1024,640]{0,1:T(8,128)(2,1)S(1)}, f32[1024,640]{0,1:T(8,128)}, f32[1024,640]{0,1:T(8,128)}) fusion(f32[1024,2,640]{0,2,1:T(8,128)} %convolution_bitcast_fusion.1, f32[1024,1920]{0,1:T(8,128)} %convolution_bitcast_fusion), kind=kLoop, calls=%fused_computation.48 | loop fusion | flops 3276800 | bytes 19660800 | tf_op jit(solution)/shard_map/convert_element_type | solution.py:117
  271.1 2.7 copy.70
  273.8 3.7 reshape.153
  277.5 4.8 %reshape.152 = f32[2,512,5,128]{1,0,3,2:T(2,128)} reshape(f32[1024,640]{0,1:T(8,128)} %get-tuple-element.96) | data formatting | bytes 5242880 | tf_op jit(solution)/shard_map/reshape | solution.py:112
  282.3 2.2 copy.59
  286.8 2.7 fusion.48
  289.5 25.5 %while.12 = (s32[]{:T(128)}, f32[2,512,5,128]{1,3,2,0:T(8,128)}, bf16[2,512,5,128]{1,3,2,0:T(8,128)(2,1)}, bf16[2,512,5,128]{1,3,2,0:T(8,128)(2,1)}, s32[2]{0:T(...) while((s32[]{:T(128)}, f32[2,512,5,128]{1,3,2,0:T(8,128)}, ...), condition=%wide.region_4.5_spmd, body=%wide.region_0.4_spmd.sunk | while | flops 1362688512 | bytes 96298296 | solution.py:124
  291.0 2.2 fusion.104
  293.2 2.5 fusion.106
  300.8 1.4 copy-done.5
  303.7 2.2 fusion.104
  305.9 2.5 fusion.106
  313.5 1.4 copy-done.5
  315.0 2.6 copy.72
  318.2 1.8 fusion.49
  320.0 1.8 copy.71
  323.1 14.2 %psum.14 = bf16[2,512,2,8]{1,3,2,0:T(8,128)(2,1)S(1)} all-reduce(f32[2,512,2,8]{1,3,2,0:T(8,128)S(1)} %fusion.65), channel_id=1, replica_groups=mesh['dp'=32,'tensor'=4] {'tensor'}, use_global_device_ids=true, to_apply=%region_5.6 | all-reduce | flops 16384 | bytes 98304 | tf_op jit(solution)/shard_map/psum | solution.py:137
  338.2 3.3 fusion.61
  342.6 3.8 all-to-all-start
  346.5 3.5 reshape.160
  350.0 3.9 all-to-all-done
  354.0 3.6 fusion.69
  359.4 3.9 all-to-all-start.1
  363.3 9.2 %all-to-all-done.1 = bf16[32,2,4096]{2,1,0:T(2,128)(2,1)S(1)} async-done(((bf16[32,2,4096]{2,1,0:T(2,128)(2,1)}), bf16[32,2,4096]{2,1,0:T(2,128)(2,1)S(1)}, u32[]{:S(2)}, u32[]{:S(2)}) %all-to-all-start.1) | async-done | bytes 524320 | tf_op jit(solution)/shard_map/all_to_all | solution.py:170
  372.9 17.3 %psum.15 = f32[2,4096]{1,0:T(2,128)S(1)} all-reduce(f32[2,4096]{1,0:T(2,128)S(1)} %convert_reduce_fusion), channel_id=1, replica_groups=mesh['dp'=32,'tensor'=4] {'tensor'}, use_global_device_ids=true, to_apply=%region_7.8 | all-reduce | flops 8192 | bytes 65536 | tf_op jit(solution)/shard_map/psum | solution.py:175
  (89 shorter events, 25.3 us)
Async XLA Ops:
  6.5 18.6 %copy-start = (bf16[2,8,5120]{2,1,0:T(8,128)(2,1)S(1)}, bf16[2,8,5120]{2,1,0:T(8,128)(2,1)}, u32[]{:S(2)}) copy-start(bf16[2,8,5120]{2,1,0:T(8,128)(2,1)} %param.16) | copy-start | bytes 491524
  6.5 2.1 copy-start.7
  6.5 226.0 %all-gather.2.cloned.1.call-start = ((), (), s32[]{:S(2)}) async-start(), calls=%async_computation.2 | async-start | bytes 20275200 | tf_op jit(solution)/shard_map/all_gather | solution.py:94
  9.4 14.5 %copy-start.17 = (s32[2]{0:T(128)S(1)}, s32[2]{0:T(128)}, u32[]{:S(2)}) copy-start(s32[2]{0:T(128)} %param.19) | copy-start | bytes 28
  25.1 7.4 %copy-start.15 = (bf16[2,8,640]{2,1,0:T(8,128)(2,1)S(1)}, bf16[2,8,640]{2,1,0:T(8,128)(2,1)}, u32[]{:S(2)}) copy-start(bf16[2,8,640]{2,1,0:T(8,128)(2,1)} %param.17) | copy-start | bytes 61444
  31.9 0.6 copy-start.13
  285.1 1.7 copy-start.2
  293.1 2.6 copy-start.9
  293.2 2.6 copy-start.12
  295.7 1.3 copy-start.8
  297.0 1.1 copy-start.10
  297.0 1.8 copy-start.3
  297.0 2.6 copy-start.4
  300.8 1.5 copy-start.5
  305.9 2.6 copy-start.9
  305.9 2.6 copy-start.12
  308.5 1.3 copy-start.8
  309.8 1.1 copy-start.10
  309.8 1.8 copy-start.3
  309.8 2.6 copy-start.4
  313.5 1.5 copy-start.5
  315.0 2.6 copy-start.6
  320.0 1.8 copy-start.11
  320.0 1.8 copy-start.16
  321.9 0.8 copy-start.14
  342.6 11.3 %all-to-all-start = ((bf16[2,32,1,960]{3,0,2,1:T(2,128)(2,1)}), bf16[2,32,1,960]{3,0,2,1:T(2,128)(2,1)S(1)}, u32[]{:S(2)}, u32[]{:S(2)}) async-start(bf16[2,32,1,960]{3,0,2,1:T(2,128)(2,1)} %pad_maximum_fusion.12), calls=%async_computation | async-start | bytes 262144 | tf_op jit(solution)/shard_map/all_to_all | solution.py:160
  354.0 37.1 %copy-start.1 = (bf16[2,8,5120]{2,1,0:T(8,128)(2,1)S(1)}, bf16[2,8,5120]{2,1,0:T(8,128)(2,1)}, u32[]{:S(2)}) copy-start(bf16[2,8,5120]{2,1,0:T(8,128)(2,1)} %param.16) | copy-start | bytes 491524
  359.4 13.1 %all-to-all-start.1 = ((bf16[32,2,4096]{2,1,0:T(2,128)(2,1)}), bf16[32,2,4096]{2,1,0:T(2,128)(2,1)S(1)}, u32[]{:S(2)}, u32[]{:S(2)}) async-start(bf16[32,2,4096]{2,1,0:T(2,128)(2,1)} %reshape.161), calls=%async_computation.1 | async-start | bytes 1048576 | tf_op jit(solution)/shard_map/all_to_all | solution.py:170
Sparse Core Ops, SparseCore 0:
  9.0 223.5 all-gather.1

commit v3 on v2

--- a/solution.py
+++ b/solution.py
@@ -1,11 +1,13 @@
 import jax
 import jax.numpy as jnp
 from jax import lax
-from jax.sharding import PartitionSpec as P
+from jax.sharding import Mesh, PartitionSpec as P
 
 HEAD_DIM = 128
 ADAPTER_RANK = 8
 FEAT = 4096
+DP_AXES = ("zl", "x", "y")
+TP_AXES = ("zh", "core")
 
 
 adapter_scale = 2.0
@@ -87,11 +89,21 @@
     def add_rows(weight_piece):
         return jnp.dot(token_matrix, weight_piece, preferred_element_type=jnp.float32)
 
-    parts_dp = lax.axis_size("dp")
+    parts_dp = lax.axis_size(DP_AXES)
     local_rows = jnp.concatenate(
         [query_projection_matrix, key_projection_matrix, value_projection_matrix], axis=1
     )
-    all_rows = lax.all_gather(local_rows, "dp", axis=0, tiled=True)
+    partner_rows = lax.ppermute(local_rows, "zl", [(0, 1), (1, 0)])
+    low_first = lax.axis_index("zl") == 0
+    pair_rows = jnp.stack(
+        [
+            jnp.where(low_first, local_rows, partner_rows),
+            jnp.where(low_first, partner_rows, local_rows),
+        ]
+    )
+    all_rows = lax.all_gather(pair_rows, ("x", "y"), axis=1, tiled=False).reshape(
+        -1, local_rows.shape[1]
+    )
     projected = add_rows(all_rows)
     plain_query = projected[:, :local_cols]
     base_key = projected[:, local_cols : 2 * local_cols]
@@ -134,16 +146,16 @@
     branch_portion = jnp.einsum(
         "liov,ohv->lioh", per_head_gradient, adapter_up_maps, preferred_element_type=jnp.float32
     )
-    adapter_branch = lax.psum(branch_portion, "tensor").astype(jnp.bfloat16)
+    adapter_branch = lax.psum(branch_portion, TP_AXES).astype(jnp.bfloat16)
     middle_seq = inner_hidden.reshape(seq_count, seq_len, 2, ADAPTER_RANK)
     up_map_gradient = adapter_scale * jnp.einsum(
         "esar,esac->earc", middle_seq, per_head_gradient, preferred_element_type=jnp.float32
     )
-    parts_tensor = lax.axis_size("tensor")
+    parts_tensor = lax.axis_size(TP_AXES)
     row_block = model_width // (parts_dp * parts_tensor)
     hidden_blocks = hidden.reshape(seq_count, seq_len, parts_dp, parts_tensor, row_block)
     local_column_range = lax.dynamic_index_in_dim(
-        hidden_blocks, lax.axis_index("tensor"), axis=3, keepdims=False
+        hidden_blocks, lax.axis_index(TP_AXES), axis=3, keepdims=False
     )
     down_map_local = adapter_scale * jnp.einsum(
         "ykzu,ykhc->yhzuc", adapter_branch, local_column_range, preferred_element_type=jnp.float32
@@ -157,7 +169,7 @@
         seq_count, parts_dp, 1, 2 * ADAPTER_RANK * heads_local * slice_len
     )
     packed = jnp.concatenate([down_map_local, up_blocks], axis=3).astype(jnp.bfloat16)
-    routed = lax.all_to_all(packed, "dp", split_axis=1, concat_axis=0, tiled=True)
+    routed = lax.all_to_all(packed, DP_AXES, split_axis=1, concat_axis=0, tiled=True)
     gathered = routed.reshape(routed.shape[0], routed.shape[3])
     down_count = down_map_local.shape[3]
     down_table = random_signs_down.reshape(down_count, random_signs_down.shape[-1])
@@ -168,34 +180,35 @@
     ).astype(jnp.bfloat16)
     own_count = partial.shape[0] // parts_dp
     to_owner = lax.all_to_all(
-        partial.reshape(parts_dp, own_count, partial.shape[1]), "dp", 0, 0, tiled=True
+        partial.reshape(parts_dp, own_count, partial.shape[1]), DP_AXES, 0, 0, tiled=True
     )
     own_rows = jnp.sum(to_owner.astype(jnp.float32), axis=0)
     feat_block = own_rows.shape[1] // parts_tensor
-    full_rows = lax.psum(own_rows, "tensor")
+    full_rows = lax.psum(own_rows, TP_AXES)
     squares = jnp.sum(full_rows * full_rows, axis=1)
     features_local = lax.dynamic_slice_in_dim(
-        full_rows, lax.axis_index("tensor") * feat_block, feat_block, axis=1
+        full_rows, lax.axis_index(TP_AXES) * feat_block, feat_block, axis=1
     )
     return features_local * lax.rsqrt(squares / FEAT + norm_eps)[:, None]
 
 
 def solution(mesh):
+    fine_mesh = Mesh(mesh.devices.reshape(2, 4, 4, 2, 2), ("zl", "x", "y", "zh", "core"))
     return jax.shard_map(
         body,
-        mesh=mesh,
+        mesh=fine_mesh,
         in_specs=(
-            P("dp", None, None),
-            P("dp", "tensor"),
-            P("dp", "tensor"),
-            P("dp", "tensor"),
+            P(DP_AXES, None, None),
+            P(DP_AXES, TP_AXES),
+            P(DP_AXES, TP_AXES),
+            P(DP_AXES, TP_AXES),
             P(),
-            P(None, None, "tensor"),
-            P("dp", None, "tensor"),
-            P("dp"),
-            P(None, None, ("dp", "tensor"), None),
-            P(None, None, "tensor", "dp", None),
+            P(None, None, TP_AXES),
+            P(DP_AXES, None, TP_AXES),
+            P(DP_AXES),
+            P(None, None, DP_AXES + TP_AXES, None),
+            P(None, None, TP_AXES, DP_AXES, None),
         ),
-        out_specs=P("dp", "tensor"),
+        out_specs=P(DP_AXES, TP_AXES),
         check_vma=False,
     )

time: 399 us -> 332 us (0.83)
  waiting for transfers between devices: 210 us -> 128 us
  starting transfers between devices: 7.73 us -> 12.6 us
    all_gather x1, waiting for transfers between devices: 197 us -> 101 us  [body(): lax.all_gather(pair_rows, ('x', 'y'), axis=1, tiled=False)]
    ppermute x0 -> x1, waiting for transfers between devices: none -> 13.6 us  [body(): partner_rows = lax.ppermute(local_rows, 'zl', [(0, 1), (1, 0)])]
    while x28 -> x20, local copies, waits for them, and re-layouts: 7.03 us -> 1.83 us
    reshape x2, local copies, waits for them, and re-layouts: 4.16 us -> 8.6 us  [body(): (plain_query + adapter_scale * raised_features[:, 0]).reshape(head_layout)]
    unnamed x24 -> x28, local copies, waits for them, and re-layouts: 15.9 us -> 17.2 us
  transfers between devices with their start and end apart: 3 -> 4, of which waited for: 3 -> 4; matrix products, arithmetic and copies ran while one was open for 8% -> 9% of each run, Pallas kernels for 0% -> 0%
where the time goes in v3:
time: 332 us; the launch traced here: 331 us
  waiting for transfers between devices  128 us (39%)
  matrix products  60.9 us (18%)
  local copies, waits for them, and re-layouts  52.9 us (16%)
  blocking collectives  31.4 us (9%)
  other arithmetic  31.2 us (9%)
  between operations  13.7 us (4%)
  starting transfers between devices  12.6 us (4%)
    all_gather x1, waiting for transfers between devices, body(): lax.all_gather(pair_rows, ('x', 'y'), axis=1, tiled=False)  101 us
    dot_general x1, matrix products, add_rows(): jnp.dot(token_matrix, weight_piece, preferred_element_type=jnp.float32)  28.4 us
    psum x1, blocking collectives, body(): full_rows = lax.psum(own_rows, TP_AXES)  17.2 us
    unnamed x28, local copies, waits for them, and re-layouts  17.2 us
    psum x1, blocking collectives, body(): adapter_branch = lax.psum(branch_portion, TP_AXES).astype(jnp.bfloat16)  14.2 us
    ppermute x1, waiting for transfers between devices, body(): partner_rows = lax.ppermute(local_rows, 'zl', [(0, 1), (1, 0)])  13.6 us
    all_to_all x1, waiting for transfers between devices, body(): lax.all_to_all(partial.reshape(parts_dp, own_count, partial.shape[1]), DP...  9.19 us
    convert_element_type x1, other arithmetic, body(): value_per_head = (plain_value + adapter_scale * raised_features[:, 1]).as...  8.61 us
  transfers between devices with their start and end apart: 4, of which 4 were waited for; matrix products, arithmetic and copies ran while one was open for 9% of the time, Pallas kernels for 0%

profile of v3, /device:TPU:1, one launch (start us, length us, event | category | flops | bytes accessed | tf_op | source)
XLA Modules:
  0.0 330.9 jit_solution(1883115923209386000)
XLA Ops:
  9.4 2.5 collective-permute-start
  12.0 13.6 %collective-permute-done = bf16[160,1920]{1,0:T(8,128)(2,1)S(1)} collective-permute-done((bf16[160,1920]{1,0:T(8,128)(2,1)S(1)}, bf16[160,1920]{1,0:T(8,128)(2,1)S(1)}, u32[]{:S(2)}, u32[]{:S(2)}) %collective-permute-start) | collective-permute-done | bytes 614432 | tf_op jit(solution)/shard_map/ppermute | solution.py:96
  27.6 13.9 %copy.58 = bf16[2,512,5120]{1,2,0:T(8,128)(2,1)} copy(bf16[2,512,5120]{2,1,0:T(8,128)(2,1)} %param.12) | data formatting | bytes 20971520 | tf_op args[0]
  43.4 6.8 %convolution_convert_fusion = bf16[1024,2,8]{0,2,1:T(8,128)(2,1)S(1)} fusion(bf16[1024,5120,1]{1,0,2:T(8,128)(2,1)} %bitcast.133, bf16[2,8,5120]{2,1,0:T(8,128)(2,1)S(1)} %copy-done), kind=kOutput, calls=%fused_computation.79 | convolution fusion | flops 167788544 | bytes 10682368 | tf_op jit(solution)/shard_map/no,wio->nwi/dot_general | solution.py:112
  50.8 3.2 convolution_bitcast_fusion.1
  54.0 101.4 %all-gather.3.cloned.1.call-done = bf16[2,2560,1920]{2,1,0:T(8,128)(2,1)} async-done(((bf16[2,160,1920]{2,1,0:T(8,128)(2,1)}), bf16[2,2560,1920]{2,1,0:T(8,128)(2,1)}) %all-gather.3.cloned.1.call-update) | async-done | bytes 19660816 | tf_op jit(solution)/shard_map/all_gather | solution.py:104
  155.4 28.4 %convolution_bitcast_fusion = f32[1024,1920]{0,1:T(8,128)} fusion(bf16[5120,1920]{1,0:T(8,128)(2,1)} %bitcast.144, bf16[1024,5120]{1,0:T(8,128)(2,1)} %bitcast.134), kind=kOutput, calls=%fused_computation.44 | convolution fusion | flops 20132659200 | bytes 38010880 | tf_op jit(solution)/shard_map/dot_general | solution.py:90
  183.8 8.6 %fusion.42 = (bf16[1024,640]{0,1:T(8,128)(2,1)}, f32[1024,640]{0,1:T(8,128)}, f32[1024,640]{0,1:T(8,128)}) fusion(f32[1024,2,640]{0,2,1:T(8,128)} %convolution_bitcast_fusion.1, f32[1024,1920]{0,1:T(8,128)} %convolution_bitcast_fusion), kind=kLoop, calls=%fused_computation.48 | loop fusion | flops 3276800 | bytes 19660800 | tf_op jit(solution)/shard_map/convert_element_type | solution.py:129
  192.4 3.7 %reshape.156 = f32[2,512,5,128]{1,0,3,2:T(2,128)S(1)} reshape(f32[1024,640]{0,1:T(8,128)} %get-tuple-element.96) | data formatting | bytes 5242880 | tf_op jit(solution)/shard_map/reshape | solution.py:124
  198.0 4.8 %reshape.157 = f32[2,512,5,128]{1,0,3,2:T(2,128)} reshape(f32[1024,640]{0,1:T(8,128)} %get-tuple-element.95) | data formatting | bytes 5242880 | tf_op jit(solution)/shard_map/reshape | solution.py:120
  202.8 3.8 %copy.63 = f32[2,512,5,128]{1,3,2,0:T(8,128)} copy(f32[2,512,5,128]{1,0,3,2:T(2,128)} %reshape.157) | data formatting | bytes 5242880 | tf_op jit(solution)/shard_map/reshape | solution.py:120
  206.6 4.4 %reshape.159 = bf16[2,512,5,128]{1,0,3,2:T(2,128)(2,1)} reshape(bf16[1024,640]{0,1:T(8,128)(2,1)} %get-tuple-element.94) | data formatting | bytes 2621440 | tf_op jit(solution)/shard_map/reshape | solution.py:130
  211.0 4.3 %copy.70 = bf16[2,512,5,128]{3,1,2,0:T(8,128)(2,1)} copy(bf16[2,512,5,128]{1,0,3,2:T(2,128)(2,1)} %reshape.159) | data formatting | bytes 2621440 | tf_op jit(solution)/shard_map/while | solution.py:136
  215.3 3.4 %slice_negate_fusion.1 = (f32[2,512,5,64]{1,3,2,0:T(8,128)S(1)}, f32[2,512,5,64]{1,3,2,0:T(8,128)S(1)}, f32[2,512,5,64]{1,3,2,0:T(8,128)S(1)}, f32[2,512,5,64]{1,3,2,0:T(8,128)S(1)}) fusion(f32[2,512,5,128]{1,3,2,0:T(8,128)} %copy.63, f32[2,512,5,128]{1,3,2,0:T(8,128)} %copy.59), kind=kLoop, calls=%fused_computation.68 | loop fusion | flops 655360 | bytes 10485760 | tf_op jit(solution)/shard_map/neg | solution.py:30
  218.7 2.7 fusion.48
  221.4 22.2 %while.12 = (s32[]{:T(128)}, f32[2,512,5,128]{1,3,2,0:T(8,128)}, bf16[2,512,5,128]{1,3,2,0:T(8,128)(2,1)}, bf16[2,512,5,128]{1,3,2,0:T(8,128)(2,1)}, s32[2]{0:T(...) while((s32[]{:T(128)}, f32[2,512,5,128]{1,3,2,0:T(8,128)}, ...), condition=%wide.region_4.5_spmd, body=%wide.region_0.4_spmd.sunk | while | flops 1362688512 | bytes 75326712 | solution.py:136
  221.4 2.2 fusion.104
  224.9 2.5 fusion.106
  230.3 2.2 fusion.107
  232.5 2.2 fusion.104
  236.1 2.5 fusion.106
  241.4 2.2 fusion.107
  246.0 2.5 fusion.49
  253.5 14.2 %psum.14 = bf16[2,512,2,8]{1,3,2,0:T(8,128)(2,1)S(1)} all-reduce(f32[2,512,2,8]{1,3,2,0:T(8,128)S(1)} %fusion.65), channel_id=1, replica_groups=mesh['zl'=2,'x'=4,'y'=4,'zh'=2,'core'=2] {'zh','core'}, use_global_device_ids=true, to_apply=%region_5.6 | all-reduce | flops 16384 | bytes 98304 | tf_op jit(solution)/shard_map/psum | solution.py:149
  267.7 3.3 fusion.61
  273.5 6.1 %all-to-all-start = ((bf16[2,32,1,960]{3,0,2,1:T(2,128)(2,1)}), bf16[2,32,1,960]{3,0,2,1:T(2,128)(2,1)S(1)}, u32[]{:S(2)}, u32[]{:S(2)}) async-start(bf16[2,32,1,960]{3,0,2,1:T(2,128)(2,1)} %pad_maximum_fusion.12), calls=%async_computation | async-start | bytes 262144 | tf_op jit(solution)/shard_map/all_to_all | solution.py:172
  279.6 3.5 %reshape.164 = bf16[320,4096]{1,0:T(8,128)(2,1)S(1)} reshape(bf16[2,8,5,4,4096]{4,3,2,1,0:T(4,128)(2,1)} %param.21) | data formatting | bytes 5242880 | tf_op jit(solution)/shard_map/reshape | solution.py:176
  283.2 3.9 %all-to-all-done = bf16[2,32,1,960]{3,0,2,1:T(2,128)(2,1)S(1)} async-done(((bf16[2,32,1,960]{3,0,2,1:T(2,128)(2,1)}), bf16[2,32,1,960]{3,0,2,1:T(2,128)(2,1)S(1)}, u32[]{:S(2)}, u32[]{:S(2)}) %all-to-all-start) | async-done | bytes 122912 | tf_op jit(solution)/shard_map/all_to_all | solution.py:172
  287.1 3.6 %fusion.69 = f32[64,4096]{1,0:T(8,128)S(1)} fusion(bf16[640,4096]{1,0:T(8,128)(2,1)} %bitcast.136, bf16[64,960]{1,0:T(8,128)(2,1)S(1)} %reshape.162), kind=kOutput, calls=%fused_computation.89 | convolution fusion | flops 335544320 | bytes 6373376 | tf_op jit(solution)/shard_map/dot_general | solution.py:178
  292.5 3.9 %all-to-all-start.1 = ((bf16[32,2,4096]{2,1,0:T(2,128)(2,1)}), bf16[32,2,4096]{2,1,0:T(2,128)(2,1)S(1)}, u32[]{:S(2)}, u32[]{:S(2)}) async-start(bf16[32,2,4096]{2,1,0:T(2,128)(2,1)} %reshape.165), calls=%async_computation.1 | async-start | bytes 1048576 | tf_op jit(solution)/shard_map/all_to_all | solution.py:182
  296.4 9.2 %all-to-all-done.1 = bf16[32,2,4096]{2,1,0:T(2,128)(2,1)S(1)} async-done(((bf16[32,2,4096]{2,1,0:T(2,128)(2,1)}), bf16[32,2,4096]{2,1,0:T(2,128)(2,1)S(1)}, u32[]{:S(2)}, u32[]{:S(2)}) %all-to-all-start.1) | async-done | bytes 524320 | tf_op jit(solution)/shard_map/all_to_all | solution.py:182
  306.1 17.2 %psum.15 = f32[2,4096]{1,0:T(2,128)S(1)} all-reduce(f32[2,4096]{1,0:T(2,128)S(1)} %convert_reduce_fusion), channel_id=1, replica_groups=mesh['zl'=2,'x'=4,'y'=4,'zh'=2,'core'=2] {'zh','core'}, use_global_device_ids=true, to_apply=%region_7.8 | all-reduce | flops 8192 | bytes 65536 | tf_op jit(solution)/shard_map/psum | solution.py:187
  (89 shorter events, 30.6 us)
Async XLA Ops:
  6.5 36.8 %copy-start = (bf16[2,8,5120]{2,1,0:T(8,128)(2,1)S(1)}, bf16[2,8,5120]{2,1,0:T(8,128)(2,1)}, u32[]{:S(2)}) copy-start(bf16[2,8,5120]{2,1,0:T(8,128)(2,1)} %param.16) | copy-start | bytes 491524
  6.5 148.9 %all-gather.3.cloned.1.call-start = ((), (), s32[]{:S(2)}) async-start(), calls=%async_computation.2 | async-start | bytes 20889600 | tf_op jit(solution)/shard_map/all_gather | solution.py:104
  9.4 16.1 %collective-permute-start = (bf16[160,1920]{1,0:T(8,128)(2,1)S(1)}, bf16[160,1920]{1,0:T(8,128)(2,1)S(1)}, u32[]{:S(2)}, u32[]{:S(2)}) collective-permute-start(bf16[160,1920]{1,0:T(8,128)(2,1)S(1)} %constant_dynamic-update-slice_fusion), channel_id=1, source_target_pairs={{0,64},{64,0},{1,65},{65,1},{2,66},{66,2},{3,67},{67,3},{4,68},{68... | collective-permute-start | bytes 1843208 | tf_op jit(solution)/shard_map/ppermute | solution.py:96
  12.0 14.9 %copy-start.4 = (bf16[2,512,640]{2,1,0:T(8,128)(2,1)S(1)}, bf16[2,512,640]{2,1,0:T(8,128)(2,1)}, u32[]{:S(2)}) copy-start(bf16[2,512,640]{2,1,0:T(8,128)(2,1)} %param.18) | copy-start | bytes 3932164
  27.6 14.6 %copy-start.16 = (s32[2]{0:T(128)S(1)}, s32[2]{0:T(128)}, u32[]{:S(2)}) copy-start(s32[2]{0:T(128)} %param.19) | copy-start | bytes 28
  43.4 7.4 %copy-start.14 = (bf16[2,8,640]{2,1,0:T(8,128)(2,1)S(1)}, bf16[2,8,640]{2,1,0:T(8,128)(2,1)}, u32[]{:S(2)}) copy-start(bf16[2,8,640]{2,1,0:T(8,128)(2,1)} %param.17) | copy-start | bytes 61444
  50.2 0.6 copy-start.12
  215.3 3.4 %copy-start.2 = (f32[2,512,5,128]{1,0,3,2:T(2,128)S(1)}, f32[2,512,5,128]{1,0,3,2:T(2,128)}, u32[]{:S(2)}) copy-start(f32[2,512,5,128]{1,0,3,2:T(2,128)} %reshape.157) | copy-start | bytes 7864324
  224.9 2.6 copy-start.5
  224.9 2.6 copy-start.11
  227.5 1.3 copy-start.8
  228.5 1.2 copy-start.6
  228.8 1.5 copy-start.3
  236.0 2.6 copy-start.5
  236.0 2.6 copy-start.11
  238.6 1.3 copy-start.8
  239.6 1.2 copy-start.6
  239.9 1.5 copy-start.3
  248.4 1.5 copy-start.7
  248.5 2.9 copy-start.15
  249.9 1.5 copy-start.9
  253.5 17.9 %copy-start.10 = (bf16[2,512,1,640]{3,1,2,0:T(8,128)(2,1)S(1)}, bf16[2,512,1,640]{3,1,2,0:T(8,128)(2,1)}, u32[]{:S(2)}) copy-start(bf16[2,512,1,640]{3,1,2,0:T(8,128)(2,1)} %copy.72) | copy-start | bytes 3932164
  253.5 17.9 %copy-start.13 = (bf16[1024,2,8]{0,2,1:T(8,128)(2,1)S(1)}, bf16[1024,2,8]{0,2,1:T(8,128)(2,1)}, u32[]{:S(2)}) copy-start(bf16[1024,2,8]{0,2,1:T(8,128)(2,1)} %copy-done.12) | copy-start | bytes 98308
  273.5 13.6 %all-to-all-start = ((bf16[2,32,1,960]{3,0,2,1:T(2,128)(2,1)}), bf16[2,32,1,960]{3,0,2,1:T(2,128)(2,1)S(1)}, u32[]{:S(2)}, u32[]{:S(2)}) async-start(bf16[2,32,1,960]{3,0,2,1:T(2,128)(2,1)} %pad_maximum_fusion.12), calls=%async_computation | async-start | bytes 262144 | tf_op jit(solution)/shard_map/all_to_all | solution.py:172
  287.1 37.0 %copy-start.1 = (bf16[2,8,5120]{2,1,0:T(8,128)(2,1)S(1)}, bf16[2,8,5120]{2,1,0:T(8,128)(2,1)}, u32[]{:S(2)}) copy-start(bf16[2,8,5120]{2,1,0:T(8,128)(2,1)} %param.16) | copy-start | bytes 491524
  292.5 13.1 %all-to-all-start.1 = ((bf16[32,2,4096]{2,1,0:T(2,128)(2,1)}), bf16[32,2,4096]{2,1,0:T(2,128)(2,1)S(1)}, u32[]{:S(2)}, u32[]{:S(2)}) async-start(bf16[32,2,4096]{2,1,0:T(2,128)(2,1)} %reshape.165), calls=%async_computation.1 | async-start | bytes 1048576 | tf_op jit(solution)/shard_map/all_to_all | solution.py:182
Sparse Core Ops, SparseCore 0:
  27.0 128.4 all-gather.2

commit v4 on v3

--- a/solution.py
+++ b/solution.py
@@ -179,16 +179,17 @@
         + jnp.dot(gathered[:, down_count:], up_table, preferred_element_type=jnp.float32)
     ).astype(jnp.bfloat16)
     own_count = partial.shape[0] // parts_dp
+    feat_block = partial.shape[1] // parts_tensor
+    blocks = partial.reshape(parts_dp, own_count, parts_tensor, feat_block).transpose(0, 2, 1, 3)
     to_owner = lax.all_to_all(
-        partial.reshape(parts_dp, own_count, partial.shape[1]), DP_AXES, 0, 0, tiled=True
-    )
-    own_rows = jnp.sum(to_owner.astype(jnp.float32), axis=0)
-    feat_block = own_rows.shape[1] // parts_tensor
-    full_rows = lax.psum(own_rows, TP_AXES)
-    squares = jnp.sum(full_rows * full_rows, axis=1)
-    features_local = lax.dynamic_slice_in_dim(
-        full_rows, lax.axis_index(TP_AXES) * feat_block, feat_block, axis=1
-    )
+        blocks.reshape(parts_dp * parts_tensor, own_count, feat_block),
+        DP_AXES + TP_AXES,
+        0,
+        0,
+        tiled=True,
+    )
+    features_local = jnp.sum(to_owner.astype(jnp.float32), axis=0)
+    squares = lax.psum(jnp.sum(features_local * features_local, axis=1), TP_AXES)
     return features_local * lax.rsqrt(squares / FEAT + norm_eps)[:, None]
 
 

time: 332 us -> 330 us (level)
  blocking collectives: 31.4 us -> 42.4 us
  waiting for transfers between devices: 128 us -> 119 us
  starting transfers between devices: 12.6 us -> 8.66 us
    all_to_all x0 -> x1, blocking collectives: none -> 21.3 us  [body(): lax.all_to_all(blocks.reshape(parts_dp * parts_tensor, own_count, feat_bl...]
    psum x1, blocking collectives: 17.2 us -> 6.91 us  [body(): lax.psum(jnp.sum(features_local * features_local, axis=1), TP_AXES)]
    all_to_all x1 -> x0, waiting for transfers between devices: 9.19 us -> none  [body(): lax.all_to_all(partial.reshape(parts_dp, own_count, partial.shape[1]), DP...]
    all_to_all x1 -> x0, starting transfers between devices: 3.91 us -> none  [body(): lax.all_to_all(partial.reshape(parts_dp, own_count, partial.shape[1]), DP...]
  transfers between devices with their start and end apart: 4 -> 3, of which waited for: 4 -> 3; matrix products, arithmetic and copies ran while one was open for 9% -> 9% of each run, Pallas kernels for 0% -> 0%
where the time goes in v4:
time: 330 us; the launch traced here: 329 us
  waiting for transfers between devices  119 us (36%)
  matrix products  61 us (18%)
  local copies, waits for them, and re-layouts  52.7 us (16%)
  blocking collectives  42.4 us (13%)
  other arithmetic  31.3 us (9%)
  between operations  13.7 us (4%)
  starting transfers between devices  8.66 us (3%)
    all_gather x1, waiting for transfers between devices, body(): lax.all_gather(pair_rows, ('x', 'y'), axis=1, tiled=False)  101 us
    dot_general x1, matrix products, add_rows(): jnp.dot(token_matrix, weight_piece, preferred_element_type=jnp.float32)  28.5 us
    all_to_all x1, blocking collectives, body(): lax.all_to_all(blocks.reshape(parts_dp * parts_tensor, own_count, feat_bl...  21.3 us
    unnamed x28, local copies, waits for them, and re-layouts  17.2 us
    psum x1, blocking collectives, body(): adapter_branch = lax.psum(branch_portion, TP_AXES).astype(jnp.bfloat16)  14.2 us
    ppermute x1, waiting for transfers between devices, body(): partner_rows = lax.ppermute(local_rows, 'zl', [(0, 1), (1, 0)])  13.6 us
    convert_element_type x1, other arithmetic, body(): value_per_head = (plain_value + adapter_scale * raised_features[:, 1]).as...  8.62 us
    reshape x2, local copies, waits for them, and re-layouts, body(): (plain_query + adapter_scale * raised_features[:, 0]).reshape(head_layout)  8.61 us
  transfers between devices with their start and end apart: 3, of which 3 were waited for; matrix products, arithmetic and copies ran while one was open for 9% of the time, Pallas kernels for 0%

profile of v4, /device:TPU:1, one launch (start us, length us, event | category | flops | bytes accessed | tf_op | source)
XLA Modules:
  0.0 328.8 jit_solution(10572878828545164714)
XLA Ops:
  9.4 2.5 collective-permute-start
  12.0 13.6 %collective-permute-done = bf16[160,1920]{1,0:T(8,128)(2,1)S(1)} collective-permute-done((bf16[160,1920]{1,0:T(8,128)(2,1)S(1)}, bf16[160,1920]{1,0:T(8,128)(2,1)S(1)}, u32[]{:S(2)}, u32[]{:S(2)}) %collective-permute-start) | collective-permute-done | bytes 614432 | tf_op jit(solution)/shard_map/ppermute | solution.py:96
  27.6 13.9 %copy.59 = bf16[2,512,5120]{1,2,0:T(8,128)(2,1)} copy(bf16[2,512,5120]{2,1,0:T(8,128)(2,1)} %param.12) | data formatting | bytes 20971520 | tf_op args[0]
  43.4 6.8 %convolution_convert_fusion = bf16[1024,2,8]{0,2,1:T(8,128)(2,1)S(1)} fusion(bf16[1024,5120,1]{1,0,2:T(8,128)(2,1)} %bitcast.136, bf16[2,8,5120]{2,1,0:T(8,128)(2,1)S(1)} %copy-done), kind=kOutput, calls=%fused_computation.79 | convolution fusion | flops 167788544 | bytes 10682368 | tf_op jit(solution)/shard_map/no,wio->nwi/dot_general | solution.py:112
  50.8 3.2 convolution_bitcast_fusion.1
  54.0 101.4 %all-gather.3.cloned.1.call-done = bf16[2,2560,1920]{2,1,0:T(8,128)(2,1)} async-done(((bf16[2,160,1920]{2,1,0:T(8,128)(2,1)}), bf16[2,2560,1920]{2,1,0:T(8,128)(2,1)}) %all-gather.3.cloned.1.call-update) | async-done | bytes 19660816 | tf_op jit(solution)/shard_map/all_gather | solution.py:104
  155.4 28.5 %convolution_bitcast_fusion = f32[1024,1920]{0,1:T(8,128)} fusion(bf16[5120,1920]{1,0:T(8,128)(2,1)} %bitcast.148, bf16[1024,5120]{1,0:T(8,128)(2,1)} %bitcast.137), kind=kOutput, calls=%fused_computation.44 | convolution fusion | flops 20132659200 | bytes 38010880 | tf_op jit(solution)/shard_map/dot_general | solution.py:90
  184.0 8.6 %fusion.42 = (bf16[1024,640]{0,1:T(8,128)(2,1)}, f32[1024,640]{0,1:T(8,128)}, f32[1024,640]{0,1:T(8,128)}) fusion(f32[1024,2,640]{0,2,1:T(8,128)} %convolution_bitcast_fusion.1, f32[1024,1920]{0,1:T(8,128)} %convolution_bitcast_fusion), kind=kLoop, calls=%fused_computation.48 | loop fusion | flops 3276800 | bytes 19660800 | tf_op jit(solution)/shard_map/convert_element_type | solution.py:129
  192.6 3.7 %reshape.155 = f32[2,512,5,128]{1,0,3,2:T(2,128)S(1)} reshape(f32[1024,640]{0,1:T(8,128)} %get-tuple-element.96) | data formatting | bytes 5242880 | tf_op jit(solution)/shard_map/reshape | solution.py:124
  198.2 4.8 %reshape.156 = f32[2,512,5,128]{1,0,3,2:T(2,128)} reshape(f32[1024,640]{0,1:T(8,128)} %get-tuple-element.95) | data formatting | bytes 5242880 | tf_op jit(solution)/shard_map/reshape | solution.py:120
  203.0 3.8 %copy.64 = f32[2,512,5,128]{1,3,2,0:T(8,128)} copy(f32[2,512,5,128]{1,0,3,2:T(2,128)} %reshape.156) | data formatting | bytes 5242880 | tf_op jit(solution)/shard_map/reshape | solution.py:120
  206.8 4.4 %reshape.158 = bf16[2,512,5,128]{1,0,3,2:T(2,128)(2,1)} reshape(bf16[1024,640]{0,1:T(8,128)(2,1)} %get-tuple-element.94) | data formatting | bytes 2621440 | tf_op jit(solution)/shard_map/reshape | solution.py:130
  211.2 4.3 %copy.71 = bf16[2,512,5,128]{3,1,2,0:T(8,128)(2,1)} copy(bf16[2,512,5,128]{1,0,3,2:T(2,128)(2,1)} %reshape.158) | data formatting | bytes 2621440 | tf_op jit(solution)/shard_map/while | solution.py:136
  215.5 3.4 %slice_negate_fusion.1 = (f32[2,512,5,64]{1,3,2,0:T(8,128)S(1)}, f32[2,512,5,64]{1,3,2,0:T(8,128)S(1)}, f32[2,512,5,64]{1,3,2,0:T(8,128)S(1)}, f32[2,512,5,64]{1,3,2,0:T(8,128)S(1)}) fusion(f32[2,512,5,128]{1,3,2,0:T(8,128)} %copy.64, f32[2,512,5,128]{1,3,2,0:T(8,128)} %copy.60), kind=kLoop, calls=%fused_computation.68 | loop fusion | flops 655360 | bytes 10485760 | tf_op jit(solution)/shard_map/neg | solution.py:30
  218.9 2.7 fusion.48
  221.6 22.2 %while.12 = (s32[]{:T(128)}, f32[2,512,5,128]{1,3,2,0:T(8,128)}, bf16[2,512,5,128]{1,3,2,0:T(8,128)(2,1)}, bf16[2,512,5,128]{1,3,2,0:T(8,128)(2,1)}, s32[2]{0:T(...) while((s32[]{:T(128)}, f32[2,512,5,128]{1,3,2,0:T(8,128)}, ...), condition=%wide.region_4.5_spmd, body=%wide.region_0.4_spmd.sunk | while | flops 1362688512 | bytes 75326712 | solution.py:136
  221.6 2.2 fusion.104
  225.2 2.5 fusion.106
  230.5 2.2 fusion.107
  232.7 2.2 fusion.104
  236.3 2.5 fusion.106
  241.6 2.2 fusion.107
  246.2 2.5 fusion.49
  251.6 2.1 fusion.65
  253.7 14.2 %psum.14 = bf16[2,512,2,8]{1,3,2,0:T(8,128)(2,1)S(1)} all-reduce(f32[2,512,2,8]{1,3,2,0:T(8,128)S(1)} %fusion.65), channel_id=1, replica_groups=mesh['zl'=2,'x'=4,'y'=4,'zh'=2,'core'=2] {'zh','core'}, use_global_device_ids=true, to_apply=%region_5.6 | all-reduce | flops 16384 | bytes 98304 | tf_op jit(solution)/shard_map/psum | solution.py:149
  267.9 3.3 fusion.61
  273.7 6.1 %all-to-all-start = ((bf16[2,32,1,960]{3,0,2,1:T(2,128)(2,1)}), bf16[2,32,1,960]{3,0,2,1:T(2,128)(2,1)S(1)}, u32[]{:S(2)}, u32[]{:S(2)}) async-start(bf16[2,32,1,960]{3,0,2,1:T(2,128)(2,1)} %pad_maximum_fusion.12), calls=%async_computation | async-start | bytes 262144 | tf_op jit(solution)/shard_map/all_to_all | solution.py:172
  279.9 3.5 %reshape.163 = bf16[320,4096]{1,0:T(8,128)(2,1)S(1)} reshape(bf16[2,8,5,4,4096]{4,3,2,1,0:T(4,128)(2,1)} %param.21) | data formatting | bytes 5242880 | tf_op jit(solution)/shard_map/reshape | solution.py:176
  283.4 3.9 %all-to-all-done = bf16[2,32,1,960]{3,0,2,1:T(2,128)(2,1)S(1)} async-done(((bf16[2,32,1,960]{3,0,2,1:T(2,128)(2,1)}), bf16[2,32,1,960]{3,0,2,1:T(2,128)(2,1)S(1)}, u32[]{:S(2)}, u32[]{:S(2)}) %all-to-all-start) | async-done | bytes 122912 | tf_op jit(solution)/shard_map/all_to_all | solution.py:172
  287.3 3.5 %fusion.69 = f32[64,4096]{1,0:T(8,128)S(1)} fusion(bf16[640,4096]{1,0:T(8,128)(2,1)} %bitcast.139, bf16[64,960]{1,0:T(8,128)(2,1)S(1)} %reshape.161), kind=kOutput, calls=%fused_computation.89 | convolution fusion | flops 335544320 | bytes 6373376 | tf_op jit(solution)/shard_map/dot_general | solution.py:178
  292.5 21.3 %all_to_all.20 = bf16[128,2,1024]{2,1,0:T(2,128)(2,1)S(1)} all-to-all(bf16[128,2,1024]{2,1,0:T(2,128)(2,1)S(1)} %bitcast.142), channel_id=1, replica_groups=mesh['zl'=2,'x'=4,'y'=4,'zh'=2,'core'=2] {'zl','x','y','zh','core'}, dimensions={0} | all-to-all | bytes 1048576 | tf_op jit(solution)/shard_map/all_to_all | solution.py:184
  314.4 6.9 %psum.15 = f32[2]{0:T(128)S(1)} all-reduce(f32[2]{0:T(128)S(1)} %multiply_reduce_fusion.1), channel_id=1, replica_groups=mesh['zl'=2,'x'=4,'y'=4,'zh'=2,'core'=2] {'zh','core'}, use_global_device_ids=true, to_apply=%region_8.9 | all-reduce | flops 2 | bytes 16 | tf_op jit(solution)/shard_map/psum | solution.py:192
  (89 shorter events, 28.3 us)
Async XLA Ops:
  6.5 36.8 %copy-start = (bf16[2,8,5120]{2,1,0:T(8,128)(2,1)S(1)}, bf16[2,8,5120]{2,1,0:T(8,128)(2,1)}, u32[]{:S(2)}) copy-start(bf16[2,8,5120]{2,1,0:T(8,128)(2,1)} %param.16) | copy-start | bytes 491524
  6.5 148.9 %all-gather.3.cloned.1.call-start = ((), (), s32[]{:S(2)}) async-start(), calls=%async_computation.2 | async-start | bytes 20889600 | tf_op jit(solution)/shard_map/all_gather | solution.py:104
  9.4 16.1 %collective-permute-start = (bf16[160,1920]{1,0:T(8,128)(2,1)S(1)}, bf16[160,1920]{1,0:T(8,128)(2,1)S(1)}, u32[]{:S(2)}, u32[]{:S(2)}) collective-permute-start(bf16[160,1920]{1,0:T(8,128)(2,1)S(1)} %constant_dynamic-update-slice_fusion), channel_id=1, source_target_pairs={{0,64},{64,0},{1,65},{65,1},{2,66},{66,2},{3,67},{67,3},{4,68},{68... | collective-permute-start | bytes 1843208 | tf_op jit(solution)/shard_map/ppermute | solution.py:96
  12.0 14.9 %copy-start.4 = (bf16[2,512,640]{2,1,0:T(8,128)(2,1)S(1)}, bf16[2,512,640]{2,1,0:T(8,128)(2,1)}, u32[]{:S(2)}) copy-start(bf16[2,512,640]{2,1,0:T(8,128)(2,1)} %param.18) | copy-start | bytes 3932164
  27.6 14.5 %copy-start.16 = (s32[2]{0:T(128)S(1)}, s32[2]{0:T(128)}, u32[]{:S(2)}) copy-start(s32[2]{0:T(128)} %param.19) | copy-start | bytes 28
  43.4 7.4 %copy-start.14 = (bf16[2,8,640]{2,1,0:T(8,128)(2,1)S(1)}, bf16[2,8,640]{2,1,0:T(8,128)(2,1)}, u32[]{:S(2)}) copy-start(bf16[2,8,640]{2,1,0:T(8,128)(2,1)} %param.17) | copy-start | bytes 61444
  50.2 0.6 copy-start.12
  215.5 3.4 %copy-start.2 = (f32[2,512,5,128]{1,0,3,2:T(2,128)S(1)}, f32[2,512,5,128]{1,0,3,2:T(2,128)}, u32[]{:S(2)}) copy-start(f32[2,512,5,128]{1,0,3,2:T(2,128)} %reshape.156) | copy-start | bytes 7864324
  225.1 2.6 copy-start.5
  225.1 2.6 copy-start.11
  227.7 1.3 copy-start.8
  228.7 1.2 copy-start.6
  229.0 1.5 copy-start.3
  236.3 2.6 copy-start.5
  236.3 2.6 copy-start.11
  238.8 1.3 copy-start.8
  239.8 1.2 copy-start.6
  240.1 1.5 copy-start.3
  248.7 1.5 copy-start.7
  248.7 2.9 copy-start.15
  250.1 1.5 copy-start.9
  253.7 17.9 %copy-start.10 = (bf16[2,512,1,640]{3,1,2,0:T(8,128)(2,1)S(1)}, bf16[2,512,1,640]{3,1,2,0:T(8,128)(2,1)}, u32[]{:S(2)}) copy-start(bf16[2,512,1,640]{3,1,2,0:T(8,128)(2,1)} %copy.73) | copy-start | bytes 3932164
  253.7 17.9 %copy-start.13 = (bf16[1024,2,8]{0,2,1:T(8,128)(2,1)S(1)}, bf16[1024,2,8]{0,2,1:T(8,128)(2,1)}, u32[]{:S(2)}) copy-start(bf16[1024,2,8]{0,2,1:T(8,128)(2,1)} %copy-done.12) | copy-start | bytes 98308
  273.7 13.6 %all-to-all-start = ((bf16[2,32,1,960]{3,0,2,1:T(2,128)(2,1)}), bf16[2,32,1,960]{3,0,2,1:T(2,128)(2,1)S(1)}, u32[]{:S(2)}, u32[]{:S(2)}) async-start(bf16[2,32,1,960]{3,0,2,1:T(2,128)(2,1)} %pad_maximum_fusion.12), calls=%async_computation | async-start | bytes 262144 | tf_op jit(solution)/shard_map/all_to_all | solution.py:172
  290.9 31.1 %copy-start.1 = (bf16[2,8,5120]{2,1,0:T(8,128)(2,1)S(1)}, bf16[2,8,5120]{2,1,0:T(8,128)(2,1)}, u32[]{:S(2)}) copy-start(bf16[2,8,5120]{2,1,0:T(8,128)(2,1)} %param.16) | copy-start | bytes 491524
Sparse Core Ops, SparseCore 0:
  27.0 128.4 all-gather.2

commit v5 on v4

--- a/solution.py
+++ b/solution.py
@@ -146,7 +146,9 @@
     branch_portion = jnp.einsum(
         "liov,ohv->lioh", per_head_gradient, adapter_up_maps, preferred_element_type=jnp.float32
     )
-    adapter_branch = lax.psum(branch_portion, TP_AXES).astype(jnp.bfloat16)
+    adapter_branch = jnp.sum(
+        lax.all_gather(branch_portion, TP_AXES, axis=0, tiled=False), axis=0
+    ).astype(jnp.bfloat16)
     middle_seq = inner_hidden.reshape(seq_count, seq_len, 2, ADAPTER_RANK)
     up_map_gradient = adapter_scale * jnp.einsum(
         "esar,esac->earc", middle_seq, per_head_gradient, preferred_element_type=jnp.float32

time: 330 us -> 323 us (0.979)
  blocking collectives: 42.4 us -> 35 us
    psum x1 -> x0, blocking collectives: 14.2 us -> none  [body(): adapter_branch = lax.psum(branch_portion, TP_AXES).astype(jnp.bfloat16)]
    all_gather x0 -> x1, blocking collectives: none -> 8.21 us  [body(): lax.all_gather(branch_portion, TP_AXES, axis=0, tiled=False)]
where the time goes in v5:
time: 323 us; the launch traced here: 322 us
  waiting for transfers between devices  119 us (37%)
  matrix products  61 us (19%)
  local copies, waits for them, and re-layouts  52.7 us (16%)
  blocking collectives  35 us (11%)
  other arithmetic  31.3 us (10%)
  between operations  13.7 us (4%)
  starting transfers between devices  8.67 us (3%)
    all_gather x1, waiting for transfers between devices, body(): lax.all_gather(pair_rows, ('x', 'y'), axis=1, tiled=False)  101 us
    dot_general x1, matrix products, add_rows(): jnp.dot(token_matrix, weight_piece, preferred_element_type=jnp.float32)  28.5 us
    all_to_all x1, blocking collectives, body(): lax.all_to_all(blocks.reshape(parts_dp * parts_tensor, own_count, feat_bl...  19.9 us
    unnamed x28, local copies, waits for them, and re-layouts  17.2 us
    ppermute x1, waiting for transfers between devices, body(): partner_rows = lax.ppermute(local_rows, 'zl', [(0, 1), (1, 0)])  13.6 us
    convert_element_type x1, other arithmetic, body(): value_per_head = (plain_value + adapter_scale * raised_features[:, 1]).as...  8.62 us
    reshape x2, local copies, waits for them, and re-layouts, body(): (plain_query + adapter_scale * raised_features[:, 0]).reshape(head_layout)  8.61 us
    all_gather x1, blocking collectives, body(): lax.all_gather(branch_portion, TP_AXES, axis=0, tiled=False)  8.21 us
  transfers between devices with their start and end apart: 3, of which 3 were waited for; matrix products, arithmetic and copies ran while one was open for 9% of the time, Pallas kernels for 0%

profile of v5, /device:TPU:1, one launch (start us, length us, event | category | flops | bytes accessed | tf_op | source)
XLA Modules:
  0.0 321.6 jit_solution(1688211024387175101)
XLA Ops:
  9.4 2.5 collective-permute-start
  12.0 13.6 %collective-permute-done = bf16[160,1920]{1,0:T(8,128)(2,1)S(1)} collective-permute-done((bf16[160,1920]{1,0:T(8,128)(2,1)S(1)}, bf16[160,1920]{1,0:T(8,128)(2,1)S(1)}, u32[]{:S(2)}, u32[]{:S(2)}) %collective-permute-start) | collective-permute-done | bytes 614432 | tf_op jit(solution)/shard_map/ppermute | solution.py:96
  27.6 13.9 %copy.61 = bf16[2,512,5120]{1,2,0:T(8,128)(2,1)} copy(bf16[2,512,5120]{2,1,0:T(8,128)(2,1)} %param.12) | data formatting | bytes 20971520 | tf_op args[0]
  43.4 6.8 %convolution_convert_fusion = bf16[1024,2,8]{0,2,1:T(8,128)(2,1)S(1)} fusion(bf16[1024,5120,1]{1,0,2:T(8,128)(2,1)} %bitcast.140, bf16[2,8,5120]{2,1,0:T(8,128)(2,1)S(1)} %copy-done), kind=kOutput, calls=%fused_computation.79 | convolution fusion | flops 167788544 | bytes 10682368 | tf_op jit(solution)/shard_map/no,wio->nwi/dot_general | solution.py:112
  50.8 3.2 convolution_bitcast_fusion.1
  54.0 101.4 %all-gather.4.cloned.1.call-done = bf16[2,2560,1920]{2,1,0:T(8,128)(2,1)} async-done(((bf16[2,160,1920]{2,1,0:T(8,128)(2,1)}), bf16[2,2560,1920]{2,1,0:T(8,128)(2,1)}) %all-gather.4.cloned.1.call-update) | async-done | bytes 19660816 | tf_op jit(solution)/shard_map/all_gather | solution.py:104
  155.4 28.5 %convolution_bitcast_fusion = f32[1024,1920]{0,1:T(8,128)} fusion(bf16[5120,1920]{1,0:T(8,128)(2,1)} %bitcast.153, bf16[1024,5120]{1,0:T(8,128)(2,1)} %bitcast.141), kind=kOutput, calls=%fused_computation.44 | convolution fusion | flops 20132659200 | bytes 38010880 | tf_op jit(solution)/shard_map/dot_general | solution.py:90
  184.0 8.6 %fusion.42 = (bf16[1024,640]{0,1:T(8,128)(2,1)}, f32[1024,640]{0,1:T(8,128)}, f32[1024,640]{0,1:T(8,128)}) fusion(f32[1024,2,640]{0,2,1:T(8,128)} %convolution_bitcast_fusion.1, f32[1024,1920]{0,1:T(8,128)} %convolution_bitcast_fusion), kind=kLoop, calls=%fused_computation.48 | loop fusion | flops 3276800 | bytes 19660800 | tf_op jit(solution)/shard_map/convert_element_type | solution.py:129
  192.6 3.7 %reshape.155 = f32[2,512,5,128]{1,0,3,2:T(2,128)S(1)} reshape(f32[1024,640]{0,1:T(8,128)} %get-tuple-element.96) | data formatting | bytes 5242880 | tf_op jit(solution)/shard_map/reshape | solution.py:124
  198.2 4.8 %reshape.156 = f32[2,512,5,128]{1,0,3,2:T(2,128)} reshape(f32[1024,640]{0,1:T(8,128)} %get-tuple-element.95) | data formatting | bytes 5242880 | tf_op jit(solution)/shard_map/reshape | solution.py:120
  203.0 3.8 %copy.66 = f32[2,512,5,128]{1,3,2,0:T(8,128)} copy(f32[2,512,5,128]{1,0,3,2:T(2,128)} %reshape.156) | data formatting | bytes 5242880 | tf_op jit(solution)/shard_map/reshape | solution.py:120
  206.8 4.4 %reshape.158 = bf16[2,512,5,128]{1,0,3,2:T(2,128)(2,1)} reshape(bf16[1024,640]{0,1:T(8,128)(2,1)} %get-tuple-element.94) | data formatting | bytes 2621440 | tf_op jit(solution)/shard_map/reshape | solution.py:130
  211.2 4.3 %copy.73 = bf16[2,512,5,128]{3,1,2,0:T(8,128)(2,1)} copy(bf16[2,512,5,128]{1,0,3,2:T(2,128)(2,1)} %reshape.158) | data formatting | bytes 2621440 | tf_op jit(solution)/shard_map/while | solution.py:136
  215.5 3.4 %slice_negate_fusion.1 = (f32[2,512,5,64]{1,3,2,0:T(8,128)S(1)}, f32[2,512,5,64]{1,3,2,0:T(8,128)S(1)}, f32[2,512,5,64]{1,3,2,0:T(8,128)S(1)}, f32[2,512,5,64]{1,3,2,0:T(8,128)S(1)}) fusion(f32[2,512,5,128]{1,3,2,0:T(8,128)} %copy.66, f32[2,512,5,128]{1,3,2,0:T(8,128)} %copy.62), kind=kLoop, calls=%fused_computation.68 | loop fusion | flops 655360 | bytes 10485760 | tf_op jit(solution)/shard_map/neg | solution.py:30
  218.9 2.7 fusion.48
  221.6 22.2 %while.12 = (s32[]{:T(128)}, f32[2,512,5,128]{1,3,2,0:T(8,128)}, bf16[2,512,5,128]{1,3,2,0:T(8,128)(2,1)}, bf16[2,512,5,128]{1,3,2,0:T(8,128)(2,1)}, s32[2]{0:T(...) while((s32[]{:T(128)}, f32[2,512,5,128]{1,3,2,0:T(8,128)}, ...), condition=%wide.region_4.5_spmd, body=%wide.region_0.4_spmd.sunk | while | flops 1362688512 | bytes 75326712 | solution.py:136
  221.6 2.2 fusion.105
  225.2 2.5 fusion.107
  230.5 2.2 fusion.108
  232.7 2.2 fusion.105
  236.3 2.5 fusion.107
  241.6 2.2 fusion.108
  246.2 2.5 fusion.49
  251.6 2.1 convolution_bitcast_fusion.2
  253.7 8.2 %all-gather.1 = f32[8,512,2,8]{1,3,0,2:T(8,128)S(1)} all-gather(f32[2,512,2,8]{1,3,0,2:T(8,128)S(1)} %convolution_bitcast_fusion.2), channel_id=3, replica_groups=mesh['zl'=2,'x'=4,'y'=4,'zh'=2,'core'=2] {'zh','core'}, dimensions={0}, use_global_device_ids=true | all-gather | bytes 327680 | tf_op jit(solution)/shard_map/all_gather | solution.py:150
  261.9 3.3 %fusion.61 = bf16[2,32,2,8,40]{4,3,2,1,0:T(8,128)(2,1)S(1)} fusion(bf16[2,512,32,4,40]{1,4,3,2,0:T(8,128)(2,1)} %bitcast.142, s32[]{:T(128)S(6)} %select_n.24, bf16[2,512,2,8]{1,3,0,2:T(8,128)(2,1)S(1)} %reduce_sum.45), kind=kOutput, calls=%fused_computation.75 | convolution fusion | flops 42024960 | bytes 2736132 | tf_op jit(solution)/shard_map/ykzu,ykhc->yhzuc/dot_general | solution.py:162
  267.7 6.1 %all-to-all-start = ((bf16[2,32,1,960]{3,0,2,1:T(2,128)(2,1)}), bf16[2,32,1,960]{3,0,2,1:T(2,128)(2,1)S(1)}, u32[]{:S(2)}, u32[]{:S(2)}) async-start(bf16[2,32,1,960]{3,0,2,1:T(2,128)(2,1)} %pad_maximum_fusion.4), calls=%async_computation | async-start | bytes 262144 | tf_op jit(solution)/shard_map/all_to_all | solution.py:174
  273.9 3.5 %reshape.163 = bf16[320,4096]{1,0:T(8,128)(2,1)S(1)} reshape(bf16[2,8,5,4,4096]{4,3,2,1,0:T(4,128)(2,1)} %param.21) | data formatting | bytes 5242880 | tf_op jit(solution)/shard_map/reshape | solution.py:178
  277.4 4.1 %all-to-all-done = bf16[2,32,1,960]{3,0,2,1:T(2,128)(2,1)S(1)} async-done(((bf16[2,32,1,960]{3,0,2,1:T(2,128)(2,1)}), bf16[2,32,1,960]{3,0,2,1:T(2,128)(2,1)S(1)}, u32[]{:S(2)}, u32[]{:S(2)}) %all-to-all-start) | async-done | bytes 122912 | tf_op jit(solution)/shard_map/all_to_all | solution.py:174
  281.5 3.5 %fusion.72 = f32[64,4096]{1,0:T(8,128)S(1)} fusion(bf16[640,4096]{1,0:T(8,128)(2,1)} %bitcast.143, bf16[64,960]{1,0:T(8,128)(2,1)S(1)} %reshape.161), kind=kOutput, calls=%fused_computation.89 | convolution fusion | flops 335544320 | bytes 6373376 | tf_op jit(solution)/shard_map/dot_general | solution.py:180
  286.7 19.9 %all_to_all.20 = bf16[128,2,1024]{2,1,0:T(2,128)(2,1)S(1)} all-to-all(bf16[128,2,1024]{2,1,0:T(2,128)(2,1)S(1)} %bitcast.146), channel_id=1, replica_groups=mesh['zl'=2,'x'=4,'y'=4,'zh'=2,'core'=2] {'zl','x','y','zh','core'}, dimensions={0} | all-to-all | bytes 1048576 | tf_op jit(solution)/shard_map/all_to_all | solution.py:186
  307.2 6.9 %psum.7 = f32[2]{0:T(128)S(1)} all-reduce(f32[2]{0:T(128)S(1)} %multiply_reduce_fusion.1), channel_id=1, replica_groups=mesh['zl'=2,'x'=4,'y'=4,'zh'=2,'core'=2] {'zh','core'}, use_global_device_ids=true, to_apply=%region_8.9 | all-reduce | flops 2 | bytes 16 | tf_op jit(solution)/shard_map/psum | solution.py:194
  (90 shorter events, 28.3 us)
Async XLA Ops:
  6.5 36.8 %copy-start = (bf16[2,8,5120]{2,1,0:T(8,128)(2,1)S(1)}, bf16[2,8,5120]{2,1,0:T(8,128)(2,1)}, u32[]{:S(2)}) copy-start(bf16[2,8,5120]{2,1,0:T(8,128)(2,1)} %param.16) | copy-start | bytes 491524
  6.5 148.9 %all-gather.4.cloned.1.call-start = ((), (), s32[]{:S(2)}) async-start(), calls=%async_computation.2 | async-start | bytes 20889600 | tf_op jit(solution)/shard_map/all_gather | solution.py:104
  9.4 16.1 %collective-permute-start = (bf16[160,1920]{1,0:T(8,128)(2,1)S(1)}, bf16[160,1920]{1,0:T(8,128)(2,1)S(1)}, u32[]{:S(2)}, u32[]{:S(2)}) collective-permute-start(bf16[160,1920]{1,0:T(8,128)(2,1)S(1)} %constant_dynamic-update-slice_fusion), channel_id=1, source_target_pairs={{0,64},{64,0},{1,65},{65,1},{2,66},{66,2},{3,67},{67,3},{4,68},{68... | collective-permute-start | bytes 1843208 | tf_op jit(solution)/shard_map/ppermute | solution.py:96
  12.0 14.9 %copy-start.4 = (bf16[2,512,640]{2,1,0:T(8,128)(2,1)S(1)}, bf16[2,512,640]{2,1,0:T(8,128)(2,1)}, u32[]{:S(2)}) copy-start(bf16[2,512,640]{2,1,0:T(8,128)(2,1)} %param.18) | copy-start | bytes 3932164
  27.6 14.5 %copy-start.16 = (s32[2]{0:T(128)S(1)}, s32[2]{0:T(128)}, u32[]{:S(2)}) copy-start(s32[2]{0:T(128)} %param.19) | copy-start | bytes 28
  43.4 7.4 %copy-start.14 = (bf16[2,8,640]{2,1,0:T(8,128)(2,1)S(1)}, bf16[2,8,640]{2,1,0:T(8,128)(2,1)}, u32[]{:S(2)}) copy-start(bf16[2,8,640]{2,1,0:T(8,128)(2,1)} %param.17) | copy-start | bytes 61444
  50.2 0.6 copy-start.12
  215.5 3.4 %copy-start.2 = (f32[2,512,5,128]{1,0,3,2:T(2,128)S(1)}, f32[2,512,5,128]{1,0,3,2:T(2,128)}, u32[]{:S(2)}) copy-start(f32[2,512,5,128]{1,0,3,2:T(2,128)} %reshape.156) | copy-start | bytes 7864324
  225.1 2.6 copy-start.5
  225.1 2.6 copy-start.11
  227.7 1.3 copy-start.8
  228.7 1.2 copy-start.6
  229.0 1.5 copy-start.3
  236.3 2.6 copy-start.5
  236.3 2.6 copy-start.11
  238.8 1.3 copy-start.8
  239.8 1.2 copy-start.6
  240.1 1.5 copy-start.3
  248.7 1.5 copy-start.7
  248.7 2.9 copy-start.15
  250.1 1.5 copy-start.9
  253.7 11.9 %copy-start.10 = (bf16[2,512,1,640]{3,1,0,2:T(8,128)(2,1)S(1)}, bf16[2,512,1,640]{3,1,0,2:T(8,128)(2,1)}, u32[]{:S(2)}) copy-start(bf16[2,512,1,640]{3,1,0,2:T(8,128)(2,1)} %copy.75) | copy-start | bytes 3932164
  253.7 11.9 %copy-start.13 = (bf16[1024,2,8]{0,2,1:T(8,128)(2,1)S(1)}, bf16[1024,2,8]{0,2,1:T(8,128)(2,1)}, u32[]{:S(2)}) copy-start(bf16[1024,2,8]{0,2,1:T(8,128)(2,1)} %copy-done.12) | copy-start | bytes 98308
  267.7 13.7 %all-to-all-start = ((bf16[2,32,1,960]{3,0,2,1:T(2,128)(2,1)}), bf16[2,32,1,960]{3,0,2,1:T(2,128)(2,1)S(1)}, u32[]{:S(2)}, u32[]{:S(2)}) async-start(bf16[2,32,1,960]{3,0,2,1:T(2,128)(2,1)} %pad_maximum_fusion.4), calls=%async_computation | async-start | bytes 262144 | tf_op jit(solution)/shard_map/all_to_all | solution.py:174
  285.1 29.7 %copy-start.1 = (bf16[2,8,5120]{2,1,0:T(8,128)(2,1)S(1)}, bf16[2,8,5120]{2,1,0:T(8,128)(2,1)}, u32[]{:S(2)}) copy-start(bf16[2,8,5120]{2,1,0:T(8,128)(2,1)} %param.16) | copy-start | bytes 491524
Sparse Core Ops, SparseCore 0:
  27.0 128.4 all-gather.3

commit v6 on v5

--- a/solution.py
+++ b/solution.py
@@ -191,7 +191,9 @@
         tiled=True,
     )
     features_local = jnp.sum(to_owner.astype(jnp.float32), axis=0)
-    squares = lax.psum(jnp.sum(features_local * features_local, axis=1), TP_AXES)
+    squares = jnp.sum(
+        lax.all_gather(jnp.sum(features_local * features_local, axis=1), TP_AXES), axis=0
+    )
     return features_local * lax.rsqrt(squares / FEAT + norm_eps)[:, None]
 
 

time: 323 us -> 325 us (level)
  blocking collectives: 35 us -> 15.1 us
  waiting for transfers between devices: 119 us -> 131 us
  starting transfers between devices: 8.67 us -> 15.3 us
    all_to_all x1 -> x0, blocking collectives: 19.9 us -> none  [body(): lax.all_to_all(blocks.reshape(parts_dp * parts_tensor, own_count, feat_bl...]
    all_to_all x0 -> x1, waiting for transfers between devices: none -> 12.2 us  [body(): lax.all_to_all(blocks.reshape(parts_dp * parts_tensor, own_count, feat_bl...]
    psum x1 -> x0, blocking collectives: 6.91 us -> none  [body(): lax.psum(jnp.sum(features_local * features_local, axis=1), TP_AXES)]
    unnamed x0 -> x1, blocking collectives: none -> 6.88 us
    all_to_all x0 -> x1, starting transfers between devices: none -> 6.68 us  [body(): lax.all_to_all(blocks.reshape(parts_dp * parts_tensor, own_count, feat_bl...]
    unnamed x28 -> x33, local copies, waits for them, and re-layouts: 17.2 us -> 18 us
  transfers between devices with their start and end apart: 3 -> 4, of which waited for: 3 -> 4; matrix products, arithmetic and copies ran while one was open for 9% -> 9% of each run, Pallas kernels for 0% -> 0%
where the time goes in v6:
time: 325 us; the launch traced here: 323 us
  waiting for transfers between devices  131 us (40%)
  matrix products  61 us (19%)
  local copies, waits for them, and re-layouts  54.5 us (17%)
  other arithmetic  31.3 us (10%)
  starting transfers between devices  15.3 us (5%)
  blocking collectives  15.1 us (5%)
  between operations  14.3 us (4%)
    all_gather x1, waiting for transfers between devices, body(): lax.all_gather(pair_rows, ('x', 'y'), axis=1, tiled=False)  101 us
    dot_general x1, matrix products, add_rows(): jnp.dot(token_matrix, weight_piece, preferred_element_type=jnp.float32)  28.5 us
    unnamed x33, local copies, waits for them, and re-layouts  18 us
    ppermute x1, waiting for transfers between devices, body(): partner_rows = lax.ppermute(local_rows, 'zl', [(0, 1), (1, 0)])  13.6 us
    all_to_all x1, waiting for transfers between devices, body(): lax.all_to_all(blocks.reshape(parts_dp * parts_tensor, own_count, feat_bl...  12.2 us
    convert_element_type x1, other arithmetic, body(): value_per_head = (plain_value + adapter_scale * raised_features[:, 1]).as...  8.62 us
    reshape x2, local copies, waits for them, and re-layouts, body(): (plain_query + adapter_scale * raised_features[:, 0]).reshape(head_layout)  8.61 us
    all_gather x1, blocking collectives, body(): lax.all_gather(branch_portion, TP_AXES, axis=0, tiled=False)  8.21 us
  transfers between devices with their start and end apart: 4, of which 4 were waited for; matrix products, arithmetic and copies ran while one was open for 9% of the time, Pallas kernels for 0%

profile of v6, /device:TPU:1, one launch (start us, length us, event | category | flops | bytes accessed | tf_op | source)
XLA Modules:
  0.0 323.0 jit_solution(1368775738593798322)
XLA Ops:
  9.4 2.5 collective-permute-start
  12.0 13.6 %collective-permute-done = bf16[160,1920]{1,0:T(8,128)(2,1)S(1)} collective-permute-done((bf16[160,1920]{1,0:T(8,128)(2,1)S(1)}, bf16[160,1920]{1,0:T(8,128)(2,1)S(1)}, u32[]{:S(2)}, u32[]{:S(2)}) %collective-permute-start) | collective-permute-done | bytes 614432 | tf_op jit(solution)/shard_map/ppermute | solution.py:96
  27.6 13.9 %copy.61 = bf16[2,512,5120]{1,2,0:T(8,128)(2,1)} copy(bf16[2,512,5120]{2,1,0:T(8,128)(2,1)} %param.12) | data formatting | bytes 20971520 | tf_op args[0]
  43.4 6.8 %convolution_convert_fusion = bf16[1024,2,8]{0,2,1:T(8,128)(2,1)S(1)} fusion(bf16[1024,5120,1]{1,0,2:T(8,128)(2,1)} %bitcast.141, bf16[2,8,5120]{2,1,0:T(8,128)(2,1)S(1)} %copy-done), kind=kOutput, calls=%fused_computation.79 | convolution fusion | flops 167788544 | bytes 10682368 | tf_op jit(solution)/shard_map/no,wio->nwi/dot_general | solution.py:112
  50.8 3.2 convolution_bitcast_fusion.1
  54.0 101.4 %all-gather.5.cloned.1.call-done = bf16[2,2560,1920]{2,1,0:T(8,128)(2,1)} async-done(((bf16[2,160,1920]{2,1,0:T(8,128)(2,1)}), bf16[2,2560,1920]{2,1,0:T(8,128)(2,1)}) %all-gather.5.cloned.1.call-update) | async-done | bytes 19660816 | tf_op jit(solution)/shard_map/all_gather | solution.py:104
  155.4 28.5 %convolution_bitcast_fusion = f32[1024,1920]{0,1:T(8,128)} fusion(bf16[5120,1920]{1,0:T(8,128)(2,1)} %bitcast.153, bf16[1024,5120]{1,0:T(8,128)(2,1)} %bitcast.142), kind=kOutput, calls=%fused_computation.44 | convolution fusion | flops 20132659200 | bytes 38010880 | tf_op jit(solution)/shard_map/dot_general | solution.py:90
  184.0 8.6 %fusion.42 = (bf16[1024,640]{0,1:T(8,128)(2,1)}, f32[1024,640]{0,1:T(8,128)}, f32[1024,640]{0,1:T(8,128)}) fusion(f32[1024,2,640]{0,2,1:T(8,128)} %convolution_bitcast_fusion.1, f32[1024,1920]{0,1:T(8,128)} %convolution_bitcast_fusion), kind=kLoop, calls=%fused_computation.48 | loop fusion | flops 3276800 | bytes 19660800 | tf_op jit(solution)/shard_map/convert_element_type | solution.py:129
  192.6 3.7 %reshape.159 = f32[2,512,5,128]{1,0,3,2:T(2,128)S(1)} reshape(f32[1024,640]{0,1:T(8,128)} %get-tuple-element.96) | data formatting | bytes 5242880 | tf_op jit(solution)/shard_map/reshape | solution.py:124
  198.2 4.8 %reshape.160 = f32[2,512,5,128]{1,0,3,2:T(2,128)} reshape(f32[1024,640]{0,1:T(8,128)} %get-tuple-element.95) | data formatting | bytes 5242880 | tf_op jit(solution)/shard_map/reshape | solution.py:120
  203.0 3.8 %copy.66 = f32[2,512,5,128]{1,3,2,0:T(8,128)} copy(f32[2,512,5,128]{1,0,3,2:T(2,128)} %reshape.160) | data formatting | bytes 5242880 | tf_op jit(solution)/shard_map/reshape | solution.py:120
  206.8 4.4 %reshape.162 = bf16[2,512,5,128]{1,0,3,2:T(2,128)(2,1)} reshape(bf16[1024,640]{0,1:T(8,128)(2,1)} %get-tuple-element.94) | data formatting | bytes 2621440 | tf_op jit(solution)/shard_map/reshape | solution.py:130
  211.2 4.3 %copy.73 = bf16[2,512,5,128]{3,1,2,0:T(8,128)(2,1)} copy(bf16[2,512,5,128]{1,0,3,2:T(2,128)(2,1)} %reshape.162) | data formatting | bytes 2621440 | tf_op jit(solution)/shard_map/while | solution.py:136
  215.5 3.4 %slice_negate_fusion.1 = (f32[2,512,5,64]{1,3,2,0:T(8,128)S(1)}, f32[2,512,5,64]{1,3,2,0:T(8,128)S(1)}, f32[2,512,5,64]{1,3,2,0:T(8,128)S(1)}, f32[2,512,5,64]{1,3,2,0:T(8,128)S(1)}) fusion(f32[2,512,5,128]{1,3,2,0:T(8,128)} %copy.66, f32[2,512,5,128]{1,3,2,0:T(8,128)} %copy.62), kind=kLoop, calls=%fused_computation.68 | loop fusion | flops 655360 | bytes 10485760 | tf_op jit(solution)/shard_map/neg | solution.py:30
  218.9 2.7 fusion.48
  221.6 22.2 %while.12 = (s32[]{:T(128)}, f32[2,512,5,128]{1,3,2,0:T(8,128)}, bf16[2,512,5,128]{1,3,2,0:T(8,128)(2,1)}, bf16[2,512,5,128]{1,3,2,0:T(8,128)(2,1)}, s32[2]{0:T(...) while((s32[]{:T(128)}, f32[2,512,5,128]{1,3,2,0:T(8,128)}, ...), condition=%wide.region_4.5_spmd, body=%wide.region_0.4_spmd.sunk | while | flops 1362688512 | bytes 75326712 | solution.py:136
  221.6 2.2 fusion.105
  225.2 2.5 fusion.107
  230.5 2.2 fusion.108
  232.7 2.2 fusion.105
  236.3 2.5 fusion.107
  241.6 2.2 fusion.108
  246.2 2.5 fusion.49
  253.7 8.2 %all-gather.1 = f32[8,512,2,8]{1,3,0,2:T(8,128)S(1)} all-gather(f32[2,512,2,8]{1,3,0,2:T(8,128)S(1)} %convolution_bitcast_fusion.2), channel_id=3, replica_groups=mesh['zl'=2,'x'=4,'y'=4,'zh'=2,'core'=2] {'zh','core'}, dimensions={0}, use_global_device_ids=true | all-gather | bytes 327680 | tf_op jit(solution)/shard_map/all_gather | solution.py:150
  261.9 3.3 %fusion.61 = bf16[2,32,2,8,40]{4,3,2,1,0:T(8,128)(2,1)S(1)} fusion(bf16[2,512,32,4,40]{1,4,3,2,0:T(8,128)(2,1)} %bitcast.143, s32[]{:T(128)S(6)} %select_n.24, bf16[2,512,2,8]{1,3,0,2:T(8,128)(2,1)S(1)} %reduce_sum.54), kind=kOutput, calls=%fused_computation.75 | convolution fusion | flops 42024960 | bytes 2736132 | tf_op jit(solution)/shard_map/ykzu,ykhc->yhzuc/dot_general | solution.py:162
  267.7 6.1 %all-to-all-start = ((bf16[2,32,1,960]{3,0,2,1:T(2,128)(2,1)}), bf16[2,32,1,960]{3,0,2,1:T(2,128)(2,1)S(1)}, u32[]{:S(2)}, u32[]{:S(2)}) async-start(bf16[2,32,1,960]{3,0,2,1:T(2,128)(2,1)} %pad_maximum_fusion.4), calls=%async_computation | async-start | bytes 262144 | tf_op jit(solution)/shard_map/all_to_all | solution.py:174
  273.9 3.5 %reshape.167 = bf16[320,4096]{1,0:T(8,128)(2,1)S(1)} reshape(bf16[2,8,5,4,4096]{4,3,2,1,0:T(4,128)(2,1)} %param.21) | data formatting | bytes 5242880 | tf_op jit(solution)/shard_map/reshape | solution.py:178
  277.4 4.1 %all-to-all-done = bf16[2,32,1,960]{3,0,2,1:T(2,128)(2,1)S(1)} async-done(((bf16[2,32,1,960]{3,0,2,1:T(2,128)(2,1)}), bf16[2,32,1,960]{3,0,2,1:T(2,128)(2,1)S(1)}, u32[]{:S(2)}, u32[]{:S(2)}) %all-to-all-start) | async-done | bytes 122912 | tf_op jit(solution)/shard_map/all_to_all | solution.py:174
  281.5 3.5 %fusion.72 = f32[64,4096]{1,0:T(8,128)S(1)} fusion(bf16[640,4096]{1,0:T(8,128)(2,1)} %bitcast.144, bf16[64,960]{1,0:T(8,128)(2,1)S(1)} %reshape.165), kind=kOutput, calls=%fused_computation.89 | convolution fusion | flops 335544320 | bytes 6373376 | tf_op jit(solution)/shard_map/dot_general | solution.py:180
  287.5 6.7 %all-to-all-start.1 = ((bf16[128,2,1024]{2,1,0:T(2,128)(2,1)}), bf16[128,2,1024]{2,1,0:T(2,128)(2,1)S(1)}, u32[]{:S(2)}, u32[]{:S(2)}) async-start(bf16[128,2,1024]{2,1,0:T(2,128)(2,1)} %bitcast.39), calls=%async_computation.1 | async-start | bytes 1048576 | tf_op jit(solution)/shard_map/all_to_all | solution.py:186
  295.4 12.2 %all-to-all-done.1 = bf16[128,2,1024]{2,1,0:T(2,128)(2,1)S(1)} async-done(((bf16[128,2,1024]{2,1,0:T(2,128)(2,1)}), bf16[128,2,1024]{2,1,0:T(2,128)(2,1)S(1)}, u32[]{:S(2)}, u32[]{:S(2)}) %all-to-all-start.1) | async-done | bytes 524320 | tf_op jit(solution)/shard_map/all_to_all | solution.py:186
  308.5 6.9 %all-reduce = f32[8]{0:T(128)S(1)} all-reduce(f32[8]{0:T(128)S(1)} %dynamic-update-slice), channel_id=4, replica_groups=mesh['zl'=2,'x'=4,'y'=4,'zh'=2,'core'=2] {'zh','core'}, use_global_device_ids=true, to_apply=%add | all-reduce | flops 8 | bytes 64
  (98 shorter events, 32.1 us)
Async XLA Ops:
  6.5 36.8 %copy-start = (bf16[2,8,5120]{2,1,0:T(8,128)(2,1)S(1)}, bf16[2,8,5120]{2,1,0:T(8,128)(2,1)}, u32[]{:S(2)}) copy-start(bf16[2,8,5120]{2,1,0:T(8,128)(2,1)} %param.16) | copy-start | bytes 491524
  6.5 148.9 %all-gather.5.cloned.1.call-start = ((), (), s32[]{:S(2)}) async-start(), calls=%async_computation.2 | async-start | bytes 20889600 | tf_op jit(solution)/shard_map/all_gather | solution.py:104
  9.4 16.1 %collective-permute-start = (bf16[160,1920]{1,0:T(8,128)(2,1)S(1)}, bf16[160,1920]{1,0:T(8,128)(2,1)S(1)}, u32[]{:S(2)}, u32[]{:S(2)}) collective-permute-start(bf16[160,1920]{1,0:T(8,128)(2,1)S(1)} %constant_dynamic-update-slice_fusion), channel_id=1, source_target_pairs={{0,64},{64,0},{1,65},{65,1},{2,66},{66,2},{3,67},{67,3},{4,68},{68... | collective-permute-start | bytes 1843208 | tf_op jit(solution)/shard_map/ppermute | solution.py:96
  12.0 14.9 %copy-start.4 = (bf16[2,512,640]{2,1,0:T(8,128)(2,1)S(1)}, bf16[2,512,640]{2,1,0:T(8,128)(2,1)}, u32[]{:S(2)}) copy-start(bf16[2,512,640]{2,1,0:T(8,128)(2,1)} %param.18) | copy-start | bytes 3932164
  27.6 14.5 %copy-start.16 = (s32[2]{0:T(128)S(1)}, s32[2]{0:T(128)}, u32[]{:S(2)}) copy-start(s32[2]{0:T(128)} %param.19) | copy-start | bytes 28
  43.4 7.4 %copy-start.14 = (bf16[2,8,640]{2,1,0:T(8,128)(2,1)S(1)}, bf16[2,8,640]{2,1,0:T(8,128)(2,1)}, u32[]{:S(2)}) copy-start(bf16[2,8,640]{2,1,0:T(8,128)(2,1)} %param.17) | copy-start | bytes 61444
  50.2 0.6 copy-start.12
  215.5 3.4 %copy-start.2 = (f32[2,512,5,128]{1,0,3,2:T(2,128)S(1)}, f32[2,512,5,128]{1,0,3,2:T(2,128)}, u32[]{:S(2)}) copy-start(f32[2,512,5,128]{1,0,3,2:T(2,128)} %reshape.160) | copy-start | bytes 7864324
  225.1 2.6 copy-start.5
  225.1 2.6 copy-start.11
  227.7 1.3 copy-start.8
  228.7 1.2 copy-start.6
  229.0 1.5 copy-start.3
  236.3 2.6 copy-start.5
  236.3 2.6 copy-start.11
  238.8 1.3 copy-start.8
  239.8 1.2 copy-start.6
  240.1 1.5 copy-start.3
  248.7 1.5 copy-start.7
  248.7 2.9 copy-start.15
  250.1 1.5 copy-start.9
  253.7 11.9 %copy-start.10 = (bf16[2,512,1,640]{3,1,0,2:T(8,128)(2,1)S(1)}, bf16[2,512,1,640]{3,1,0,2:T(8,128)(2,1)}, u32[]{:S(2)}) copy-start(bf16[2,512,1,640]{3,1,0,2:T(8,128)(2,1)} %copy.75) | copy-start | bytes 3932164
  253.7 11.9 %copy-start.13 = (bf16[1024,2,8]{0,2,1:T(8,128)(2,1)S(1)}, bf16[1024,2,8]{0,2,1:T(8,128)(2,1)}, u32[]{:S(2)}) copy-start(bf16[1024,2,8]{0,2,1:T(8,128)(2,1)} %copy-done.12) | copy-start | bytes 98308
  267.7 13.7 %all-to-all-start = ((bf16[2,32,1,960]{3,0,2,1:T(2,128)(2,1)}), bf16[2,32,1,960]{3,0,2,1:T(2,128)(2,1)S(1)}, u32[]{:S(2)}, u32[]{:S(2)}) async-start(bf16[2,32,1,960]{3,0,2,1:T(2,128)(2,1)} %pad_maximum_fusion.4), calls=%async_computation | async-start | bytes 262144 | tf_op jit(solution)/shard_map/all_to_all | solution.py:174
  285.1 31.1 %copy-start.1 = (bf16[2,8,5120]{2,1,0:T(8,128)(2,1)S(1)}, bf16[2,8,5120]{2,1,0:T(8,128)(2,1)}, u32[]{:S(2)}) copy-start(bf16[2,8,5120]{2,1,0:T(8,128)(2,1)} %param.16) | copy-start | bytes 491524
  285.8 8.4 %copy-start.17 = (u32[128]{0:T(128)S(1)}, u32[128]{0:T(128)}, u32[]{:S(2)}) copy-start(u32[128]{0:T(128)} %constant.69) | copy-start | bytes 1540
  287.5 20.1 %all-to-all-start.1 = ((bf16[128,2,1024]{2,1,0:T(2,128)(2,1)}), bf16[128,2,1024]{2,1,0:T(2,128)(2,1)S(1)}, u32[]{:S(2)}, u32[]{:S(2)}) async-start(bf16[128,2,1024]{2,1,0:T(2,128)(2,1)} %bitcast.39), calls=%async_computation.1 | async-start | bytes 1048576 | tf_op jit(solution)/shard_map/all_to_all | solution.py:186
Sparse Core Ops, SparseCore 0:
  27.0 128.4 all-gather.4
